TPU v7x, 32 devices: a whole 2x2x4 slice. The times are simulated.
32 devices in a mesh: groups: 2 (over x), samp: 8 (over z, y), line: 2 (over core).
Axes of the slice: x: 2, y: 2, z: 4, core: 2. Of those that a mesh axis runs over, the one named last changes fastest.
Arguments:
- cube: float32 [7077888], P(('groups', 'samp', 'line')), parts along dimension 0, may hold values from -4000 to 4000
Outputs:
- details1: float32 [5308416], P(('groups', 'samp', 'line')), parts along dimension 0
- details2: float32 [1327104], P(('groups', 'samp', 'line')), parts along dimension 0
- details3: float32 [331776], P(('groups', 'samp', 'line')), parts along dimension 0
- approx: float32 [110592], P(('groups', 'samp', 'line')), parts along dimension 0
There are 2 independent parts, one for each index of `groups`. A program takes and returns all parts, laid end to end along the dimension named above; each array names one. Nothing has to cross between parts.
All inputs are finite; a program needn't handle non-finite values.
Results may differ from a plain program's by a relative error of at most 0.000088.
Values sent between devices are 32-bit elements; how exact they have to be, the bound alone decides.
A program may use at most 64 MiB of HBM per device.

v0:
```python
import functools
import jax
import jax.numpy as jnp
from jax import lax
from jax.experimental import pallas as pl
from jax.experimental.pallas import tpu as pltpu
from jax.sharding import PartitionSpec as P

BANDS = 432
LD = 32
SD = 16

MESH = pl.DeviceIdType.MESH
HIGH = lax.Precision.HIGHEST
LANES = 128


def blocks_of(bands):
    rows = [bands - start for start in range(0, bands, LANES)]
    offsets = [sum(rows[:i]) for i in range(len(rows))]
    return rows, offsets


alpha_lift = -1.586134342059924
beta_lift = -0.052980118572961
gamma_lift = 0.882911075530934
delta_lift = 0.443506852043971
scale_lift = 1.230174104914001
RIM = 4


def lift_list(values):
    evens, odds = values[0::2], values[1::2]
    odds = [o + alpha_lift * (e + f) for o, e, f in zip(odds[:-1], evens[:-1], evens[1:])]
    evens = [e + beta_lift * (o + q) for e, o, q in zip(evens[1:-1], odds[:-1], odds[1:])]
    odds = [o + gamma_lift * (e + f) for o, e, f in zip(odds[1:-1], evens[:-1], evens[1:])]
    evens = [e + delta_lift * (o + q) for e, o, q in zip(evens[1:-1], odds[:-1], odds[1:])]
    return [e * (1.0 / scale_lift) for e in evens], [o * scale_lift for o in odds[1:]]


def lift_lines(src, halo, dst, lines, width, ln):
    half = lines // 2
    for t in range(src.shape[0]):
        own = [src[t, i * width:(i + 1) * width] for i in range(lines)]
        got = [halo[t, i * width:(i + 1) * width] for i in range(RIM)]
        before = [jnp.where(ln == 0, own[RIM - i], got[i]) for i in range(RIM)]
        after = [jnp.where(ln == 0, got[i], own[lines - 2 - i]) for i in range(RIM)]
        low, high = lift_list(before + own + after)
        for i in range(half):
            dst[t, i * width:(i + 1) * width] = low[i]
            dst[t, (half + i) * width:(half + i + 1) * width] = high[i]


def rims(z, lines, width, left, right):
    for t in range(z.shape[0]):
        low = [z[t, pl.ds(s, lines, stride=width), :] for s in range(3)]
        top = [z[t, pl.ds(s, lines, stride=width), :] for s in range(width - 4, width)]
        left[t, :lines] = low[0]
        left[t, lines:] = low[0] + beta_lift * (low[1] + alpha_lift * (low[0] + low[2]))
        right[t, :lines] = top[3] + alpha_lift * top[2]
        right[t, lines:] = top[2] + beta_lift * (top[1] + alpha_lift * (top[0] + top[2]))


def lift_samples(z, from_left, from_right, lines, width, first, last, dests):
    half, n = lines // 2, width // 2
    for t in range(z.shape[0]):
        evens = [z[t, pl.ds(2 * i, lines, stride=width), :] for i in range(n)]
        odds = [z[t, pl.ds(2 * i + 1, lines, stride=width), :] for i in range(n)]
        beyond = jnp.where(last, evens[-1], from_right[t, :lines])
        odds1 = [o + alpha_lift * (e + f) for o, e, f in zip(odds, evens, evens[1:] + [beyond])]
        before = jnp.where(first, odds1[0], from_left[t, :lines] + alpha_lift * evens[0])
        evens1 = [e + beta_lift * (p + o) for e, p, o in zip(evens, [before] + odds1[:-1], odds1)]
        beyond = jnp.where(last, evens1[-1], from_right[t, lines:] + beta_lift * odds1[-1])
        odds2 = [o + gamma_lift * (e + f) for o, e, f in zip(odds1, evens1, evens1[1:] + [beyond])]
        outside = from_left[t, lines:] + beta_lift * before
        before = jnp.where(first, odds2[0], before + gamma_lift * (outside + evens1[0]))
        evens2 = [e + delta_lift * (p + o) for e, p, o in zip(evens1, [before] + odds2[:-1], odds2)]
        for i in range(n):
            low, high = evens2[i] * (1.0 / scale_lift), odds2[i] * scale_lift
            for (ref, base), value in zip(dests, (low[:half], low[half:], high[:half], high[half:])):
                ref[t, pl.ds(base + i, half, stride=n), :] = value


def split3(value):
    first = value.astype(jnp.bfloat16).astype(jnp.float32)
    rest = value - first
    second = rest.astype(jnp.bfloat16).astype(jnp.float32)
    return first, second, rest - second


def gram_kernel(samp, line, bands, lines, width, x_ref, o1_ref, o2_ref, o3_ref, o4_ref, t_ref, m, rest, corr, v1, v2, v3, z1, z2, z3, n1, n2, n3, el1, er1, el2, er2, el3, er3, fl1, fr1, fl2, fr2, fl3, fr3,
                l_send, l_recv, r_send, r_recv, xs, sums, sums_in, g, half_in,
                chunk_in, tot, s_send, s_recv, h_send, h_recv, c_send, c_recv, a_send, a_recv,
                b_send, b_recv):
    me, ln = lax.axis_index("samp"), lax.axis_index("line")
    devices = samp * line
    pixels = lines * width
    first, last = me == 0, me == samp - 1
    flat = me * line + ln
    packs = pixels // LANES
    padded = xs.shape[0]

    def peer(d):
        other = lax.rem(flat + d, devices)
        return {"samp": other // line, "line": lax.rem(other, line)}

    def line_copy(level, src, dst, tall, wide):
        rows = RIM * wide
        start = pl.multiple_of((1 - ln) * ((tall - RIM) * wide), 8)
        copy = pltpu.make_async_remote_copy(src.at[:, pl.ds(start, rows)], dst, l_send.at[level], l_recv.at[level],
                                            device_id={"line": 1 - ln}, device_id_type=MESH)
        copy.start()
        return copy

    def rim_copies(level, left, right, from_left, from_right):
        below = pltpu.make_async_remote_copy(left, from_right, r_send.at[level, 0], r_recv.at[level, 0],
                                             device_id={"samp": jnp.maximum(me - 1, 0)}, device_id_type=MESH)
        above = pltpu.make_async_remote_copy(right, from_left, r_send.at[level, 1], r_recv.at[level, 1],
                                             device_id={"samp": jnp.minimum(me + 1, samp - 1)}, device_id_type=MESH)

        @pl.when(me > 0)
        def _():
            below.start()

        @pl.when(me < samp - 1)
        def _():
            above.start()

        return below, above

    def rim_wait(pair):
        below, above = pair

        @pl.when(me > 0)
        def _():
            below.wait_send()
            above.wait_recv()

        @pl.when(me < samp - 1)
        def _():
            above.wait_send()
            below.wait_recv()

    for ref in (fl1, fr1, fl2, fr2, fl3, fr3):
        ref[...] = jnp.zeros_like(ref)
    barrier = pltpu.get_barrier_semaphore()
    for d in range(1, devices):
        pl.semaphore_signal(barrier, inc=1, device_id=peer(d), device_id_type=MESH)
    if padded > bands:
        xs[bands:, :] = jnp.zeros((padded - bands, pixels), jnp.float32)
    for q in range(packs):
        xs[0:bands, q * LANES:(q + 1) * LANES] = x_ref[pl.ds(q, bands, stride=packs), :]
    sums[...] = lax.dot_general(jnp.ones((8, pixels), jnp.float32), xs[...], (((1,), (1,)), ((), ())),
                                precision=HIGH, preferred_element_type=jnp.float32)[0:1]
    pl.semaphore_wait(barrier, devices - 1)
    copies = []
    for d in range(1, devices):
        copy = pltpu.make_async_remote_copy(sums, sums_in.at[d - 1], s_send.at[d - 1], s_recv.at[d - 1],
                                            device_id=peer(d), device_id_type=MESH)
        copy.start()
        copies.append(copy)
    sum_copies = copies
    local_mean = sums[...] / float(pixels)
    xs[...] = xs[...] - jnp.transpose(jnp.broadcast_to(local_mean, (8, padded)))[:, 0:1]
    rows, offsets = blocks_of(bands)
    for q, (count, offset) in enumerate(zip(rows, offsets)):
        g[offset:offset + count, :] = lax.dot_general(
            xs[q * LANES:q * LANES + count, :], xs[q * LANES:(q + 1) * LANES, :],
            (((1,), (1,)), ((), ())), precision=HIGH, preferred_element_type=jnp.float32)
    used = offsets[-1] + rows[-1]
    if g.shape[0] > used:
        g[used:, :] = jnp.zeros((g.shape[0] - used, LANES), jnp.float32)
    half = g.shape[0] // line
    chunk = half // samp
    copies = []
    for d in range(1, line):
        other = lax.rem(ln + d, line)
        copy = pltpu.make_async_remote_copy(
            g.at[pl.ds(pl.multiple_of(other * half, 8), half)], half_in.at[d - 1], h_send.at[d - 1],
            h_recv.at[d - 1], device_id={"line": other}, device_id_type=MESH)
        copy.start()
        copies.append(copy)
    for copy in copies:
        copy.wait()
    mine = pl.ds(pl.multiple_of(ln * half, 8), half)
    value = g[mine, :]
    for d in range(1, line):
        value = value + half_in[d - 1]
    g[mine, :] = value
    copies = []
    for d in range(1, samp):
        other = lax.rem(me + d, samp)
        copy = pltpu.make_async_remote_copy(
            g.at[pl.ds(pl.multiple_of(ln * half + other * chunk, 8), chunk)], chunk_in.at[d - 1],
            c_send.at[d - 1], c_recv.at[d - 1], device_id={"samp": other}, device_id_type=MESH)
        copy.start()
        copies.append(copy)
    for copy in sum_copies:
        copy.wait()
    total = sums[...]
    for d in range(1, devices):
        total = total + sums_in[d - 1]
    mean = total / float(pixels * devices)
    spread = jnp.concatenate([local_mean - mean] + [sums_in[d - 1] / float(pixels) - mean
                                                    for d in range(1, devices)], axis=0)
    shift = local_mean - mean
    for t in range(v1.shape[0]):
        v1[t] = jnp.transpose(xs[t * LANES:(t + 1) * LANES, :]) + shift[:, t * LANES:(t + 1) * LANES]
    lines1 = line_copy(0, v1, n1, lines, width)
    for q, (count, offset) in enumerate(zip(rows, offsets)):
        corr[offset:offset + count, :] = float(pixels) * lax.dot_general(
            spread, spread[:, q * LANES:(q + 1) * LANES], (((0,), (0,)), ((), ())), precision=HIGH,
            preferred_element_type=jnp.float32)[q * LANES:q * LANES + count]
    if g.shape[0] > used:
        corr[used:, :] = jnp.zeros((g.shape[0] - used, LANES), jnp.float32)
    lines1.wait()
    lift_lines(v1, n1, z1, lines, width, ln)
    rims(z1, lines, width, el1, er1)
    for copy in copies:
        copy.wait()
    own = pl.ds(pl.multiple_of(ln * half + me * chunk, 8), chunk)
    value = g[own, :] + corr[own, :]
    for d in range(1, samp):
        value = value + chunk_in[d - 1]
    tot[own, :] = value
    copies = []
    for d in range(1, samp):
        other = lax.rem(me + d, samp)
        copy = pltpu.make_async_remote_copy(tot.at[own], tot.at[own], a_send.at[d - 1], a_recv.at[d - 1],
                                            device_id={"samp": other}, device_id_type=MESH)
        copy.start()
        copies.append(copy)
    pair = rim_copies(0, el1, er1, fl1, fr1)
    for copy in copies:
        copy.wait()
    copies = []
    for d in range(1, line):
        other = lax.rem(ln + d, line)
        copy = pltpu.make_async_remote_copy(tot.at[mine], tot.at[mine], b_send.at[d - 1], b_recv.at[d - 1],
                                            device_id={"line": other}, device_id_type=MESH)
        copy.start()
        copies.append(copy)
    for copy in copies:
        copy.wait()
    wide = m.shape[1]
    rows, offsets = blocks_of(bands)
    diag = lax.broadcasted_iota(jnp.int32, (LANES, LANES), 0) == lax.broadcasted_iota(
        jnp.int32, (LANES, LANES), 1)
    scale = 1.0 / float(pixels * devices)
    trace = jnp.zeros((1, 1), jnp.float32)
    for q, offset in enumerate(offsets):
        size = min(LANES, rows[q])
        block = tot[offset:offset + size, :]
        kept = jnp.where(diag[:size], block, 0.0)
        trace = trace + jnp.sum(jnp.sum(kept, axis=0, keepdims=True), axis=1, keepdims=True)
    ridge = trace * scale * (0.01 / bands)
    for q, offset in enumerate(offsets):
        for b in range(q, len(rows)):
            size = min(LANES, rows[b])
            start = offset + (b - q) * LANES
            block = tot[start:start + size, :] * scale
            if b == q:
                low = jnp.where(diag[:size], block + ridge, block)
                m[q * LANES:q * LANES + size, q * LANES:(q + 1) * LANES] = low
            else:
                if size < LANES:
                    block = jnp.concatenate([block, jnp.zeros((LANES - size, LANES), jnp.float32)], axis=0)
                m[q * LANES:(q + 1) * LANES, b * LANES:(b + 1) * LANES] = jnp.transpose(block)
                m[b * LANES:b * LANES + size, q * LANES:(q + 1) * LANES] = block[:size]
    sub = lax.broadcasted_iota(jnp.int32, (8, LANES), 0)
    lane = lax.broadcasted_iota(jnp.int32, (8, LANES), 1)

    def eliminate(c):
        top = c * LANES
        span = bands - top

        def step(j, carry):
            row = pl.multiple_of(top + 8 * j, 8)
            here = m[pl.ds(row, 8), top:top + LANES]
            small = pltpu.roll(here, lax.rem(LANES - 8 * j, LANES), 1)
            columns = [jnp.broadcast_to(small[:, b:b + 1], (8, LANES)) for b in range(8)]
            d = [[jnp.broadcast_to(columns[b][a:a + 1, :], (8, LANES)) if b <= a else None
                  for b in range(8)] for a in range(8)]
            low = [[None] * 8 for _ in range(8)]
            root = [None] * 8
            for b in range(8):
                root[b] = lax.rsqrt(d[b][b])
                for a in range(b + 1, 8):
                    low[a][b] = d[a][b] * root[b]
                for a in range(b + 1, 8):
                    for e in range(b + 1, a + 1):
                        d[a][e] = d[a][e] - low[a][b] * low[e][b]
            inv = [[None] * 8 for _ in range(8)]
            for b in range(8):
                inv[b][b] = root[b]
                for a in range(b + 1, 8):
                    acc = low[a][b] * inv[b][b]
                    for e in range(b + 1, a):
                        acc = acc + low[a][e] * inv[e][b]
                    inv[a][b] = -(acc * root[a])
            wcol = []
            for b in range(8):
                col = jnp.where(sub == b, inv[b][b], 0.0)
                for a in range(b + 1, 8):
                    col = jnp.where(sub == a, inv[a][b], col)
                wcol.append(col)
            tiles = []
            for t in range(wide // LANES):
                acc = None
                panel = m[pl.ds(row, 8), t * LANES:(t + 1) * LANES]
                for b in range(8):
                    term = wcol[b] * panel[b:b + 1, :]
                    acc = term if acc is None else acc + term
                if t == c:
                    for b in range(8):
                        acc = jnp.where(lane == 8 * j + b, wcol[b], acc)
                tiles.append(acc)
            r = jnp.concatenate(tiles, axis=1)
            m[pl.ds(row, 8), :] = r
            one, two, three = split3(r)
            right = jnp.concatenate([one, two, three, one, two, one], axis=0)
            cols = lax.broadcasted_iota(jnp.int32, (8, wide), 1)
            keep = (cols >= row + 8).astype(jnp.float32)
            l1, l2, l3 = one * keep, two * keep, three * keep
            left = jnp.concatenate([l1, l1, l1, l2, l2, l3], axis=0)[:, top:]
            update = lax.dot_general(
                left.astype(jnp.bfloat16), right.astype(jnp.bfloat16),
                (((0,), (0,)), ((), ())), preferred_element_type=jnp.float32)
            for t in range(wide // LANES):
                part = slice(t * LANES, (t + 1) * LANES)
                old = m[top:bands, part]
                if t == c:
                    line_ids = lax.broadcasted_iota(jnp.int32, (span, LANES), 0)
                    lane_ids = lax.broadcasted_iota(jnp.int32, (span, LANES), 1)
                    inside = (lane_ids >= 8 * j) & (lane_ids < 8 * j + 8) & (line_ids >= 8 * j + 8)
                    old = jnp.where(inside, 0.0, old)
                m[top:bands, part] = old - update[:span, part]
            return carry

        lax.fori_loop(0, min(LANES, span) // 8, step, 0)
    eliminate(0)
    rim_wait(pair)
    h, w = lines // 2, width // 2
    one = h * w
    lift_samples(z1, fl1, fr1, lines, width, first, last, ((v2, 0), (t_ref, 0), (t_ref, one), (t_ref, 2 * one)))
    lines2 = line_copy(1, v2, n2, h, w)
    eliminate(1)
    lines2.wait()
    lift_lines(v2, n2, z2, h, w, ln)
    rims(z2, h, w, el2, er2)
    pair2 = rim_copies(1, el2, er2, fl2, fr2)
    eliminate(2)
    rim_wait(pair2)
    two, base2 = one // 4, 3 * one
    lift_samples(z2, fl2, fr2, h, w, first, last,
                 ((v3, 0), (t_ref, base2), (t_ref, base2 + two), (t_ref, base2 + 2 * two)))
    h, w = h // 2, w // 2
    lines3 = line_copy(2, v3, n3, h, w)
    lines3.wait()
    lift_lines(v3, n3, z3, h, w, ln)
    rims(z3, h, w, el3, er3)
    pair3 = rim_copies(2, el3, er3, fl3, fr3)
    for c in range(3, len(rows)):
        eliminate(c)
    rim_wait(pair3)
    three, base3 = two // 4, base2 + 3 * two
    lift_samples(z3, fl3, fr3, h, w, first, last,
                 ((t_ref, base3 + 3 * three), (t_ref, base3), (t_ref, base3 + three), (t_ref, base3 + 2 * three)))
    keep = lax.broadcasted_iota(jnp.int32, (bands, wide), 1) <= lax.broadcasted_iota(
        jnp.int32, (bands, wide), 0)
    m[...] = jnp.where(keep, m[...], 0.0)
    for q in range(t_ref.shape[1] // LANES):
        part = jnp.concatenate([t_ref[t, q * LANES:(q + 1) * LANES, :] for t in range(wide // LANES)], axis=1)
        out = lax.dot_general(m[...], part, (((1,), (1,)), ((), ())),
                              precision=HIGH, preferred_element_type=jnp.float32)
        if q < o1_ref.shape[0]:
            o1_ref[q] = out
        else:
            rest[...] = out


    def pack(dest, at, lane0, wide_out):
        group = LANES // wide_out
        count = bands // group
        pieces = [rest[pl.ds(b, count, stride=group), :][:, lane0:lane0 + wide_out] for b in range(group)]
        dest[at:at + count, :] = jnp.concatenate(pieces, axis=1)

    for i in range(3):
        pack(o2_ref, i * (o2_ref.shape[0] // 3), i * two, two)
        pack(o3_ref, i * (o3_ref.shape[0] // 3), 3 * two + i * three, three)
    pack(o4_ref, 0, 3 * two + 3 * three, three)


def gram_call(cube, bands, lines, width):
    pixels = lines * width
    samp, line = lax.axis_size("samp"), lax.axis_size("line")
    devices = samp * line
    rows, offsets = blocks_of(bands)
    used = offsets[-1] + rows[-1]
    unit = 8 * devices
    total = -(-used // unit) * unit
    padded = -(-bands // LANES) * LANES
    f32 = jnp.float32
    sem = pltpu.SemaphoreType.DMA
    return pl.pallas_call(
        functools.partial(gram_kernel, samp, line, bands, lines, width),
        out_shape=(jax.ShapeDtypeStruct((3, bands, LANES), f32),
                   jax.ShapeDtypeStruct((3 * bands * (pixels // 16) // LANES, LANES), f32),
                   jax.ShapeDtypeStruct((3 * bands * (pixels // 64) // LANES, LANES), f32),
                   jax.ShapeDtypeStruct((bands * (pixels // 64) // LANES, LANES), f32)),
        in_specs=[pl.BlockSpec(memory_space=pltpu.VMEM)],
        out_specs=(pl.BlockSpec(memory_space=pltpu.VMEM),) * 4,
        scratch_shapes=[
            pltpu.VMEM((padded // LANES, pixels, LANES), f32), pltpu.VMEM((bands, padded), f32),
            pltpu.VMEM((bands, LANES), f32), pltpu.VMEM((total, LANES), f32),
            *[pltpu.VMEM((padded // LANES, pixels // 4 ** i, LANES), f32) for i in (0, 1, 2)],
            *[pltpu.VMEM((padded // LANES, pixels // 4 ** i, LANES), f32) for i in (0, 1, 2)],
            *[pltpu.VMEM((padded // LANES, RIM * width // 2 ** i, LANES), f32) for i in (0, 1, 2)],
            *[pltpu.VMEM((padded // LANES, 2 * lines // 2 ** i, LANES), f32) for i in (0, 0, 1, 1, 2, 2)],
            *[pltpu.VMEM((padded // LANES, 2 * lines // 2 ** i, LANES), f32) for i in (0, 0, 1, 1, 2, 2)],
            sem((3,)), sem((3,)), sem((3, 2)), sem((3, 2)),
            pltpu.VMEM((padded, pixels), f32), pltpu.VMEM((1, padded), f32),
            pltpu.VMEM((devices - 1, 1, padded), f32), pltpu.VMEM((total, LANES), f32),
            pltpu.VMEM((line - 1, total // line, LANES), f32),
            pltpu.VMEM((samp - 1, total // devices, LANES), f32), pltpu.VMEM((total, LANES), f32),
            sem((devices - 1,)), sem((devices - 1,)), sem((line - 1,)), sem((line - 1,)),
            sem((samp - 1,)), sem((samp - 1,)), sem((samp - 1,)), sem((samp - 1,)),
            sem((line - 1,)), sem((line - 1,)),
        ],
        compiler_params=pltpu.CompilerParams(collective_id=0, has_side_effects=True),
    )(cube.reshape(-1, LANES))


def local(cube):
    return tuple(out.reshape(-1) for out in gram_call(cube, BANDS, LD, SD))


def solution(mesh):
    in_specs = (P(("groups", "samp", "line")),)
    out_specs = (
        P(("groups", "samp", "line")),
        P(("groups", "samp", "line")),
        P(("groups", "samp", "line")),
        P(("groups", "samp", "line")),
    )
    return jax.shard_map(local, mesh=mesh, in_specs=in_specs, out_specs=out_specs, check_vma=False)
```

profile of v0, /device:TPU:0, one launch (start us, length us, event | category | flops | bytes accessed | tf_op | source)
XLA Modules:
  0.0 66.0 jit_solution(4014179270629386896)
XLA Ops:
  0.6 61.2 %shard_map.46 = (f32[3,432,128]{2,1,0:T(8,128)}, f32[324,128]{1,0:T(8,128)}, f32[81,128]{1,0:T(8,128)}, f32[27,128]{1,0:T(8,128)}) custom-call(f32[1728,128]{1,0:T(8,128)} %bitcast.5), custom_call_target="tpu_custom_call" | custom-call | tf_op jit(solution)/shard_map/pallas_call | solution.py:405
  61.8 0.0 copy-start
  61.9 2.0 %copy.9 = f32[165888]{0:T(1024)} copy(f32[165888]{0:T(1024)} %bitcast.6) | data formatting | bytes 1327104
  63.9 0.0 copy-done
  63.9 0.0 copy-start.1
  63.9 0.7 %copy.10 = f32[41472]{0:T(1024)} copy(f32[41472]{0:T(1024)S(1)} %bitcast.7) | data formatting | bytes 331776
  64.6 0.1 copy-done.1
  64.7 0.0 copy-start.2
  64.7 0.6 copy.11
  65.3 0.1 copy-done.2
  65.4 0.6 copy.12
Async XLA Ops:
  61.8 2.0 %copy-start = (f32[324,128]{1,0:T(8,128)S(1)}, f32[324,128]{1,0:T(8,128)}, u32[]{:S(2)}) copy-start(f32[324,128]{1,0:T(8,128)} %get-tuple-element.9) | copy-start | bytes 497668
  63.9 0.8 %copy-start.1 = (f32[81,128]{1,0:T(8,128)S(1)}, f32[81,128]{1,0:T(8,128)}, u32[]{:S(2)}) copy-start(f32[81,128]{1,0:T(8,128)} %get-tuple-element.10) | copy-start | bytes 124420
  64.7 0.7 %copy-start.2 = (f32[27,128]{1,0:T(8,128)S(1)}, f32[27,128]{1,0:T(8,128)}, u32[]{:S(2)}) copy-start(f32[27,128]{1,0:T(8,128)} %get-tuple-element.11) | copy-start | bytes 41476
where the time goes:
time: 66.3 us; the launch traced here: 66 us
  Pallas kernels  61.2 us (92%)
  local copies, waits for them, and re-layouts  4.12 us (6%)
    pallas_call x1, Pallas kernels, gram_call(): pl.pallas_call(functools.partial(gram_kernel, samp, line, bands, lines, w...  61.2 us
    unnamed x10, local copies, waits for them, and re-layouts  4.12 us

commit v1 on v0

--- a/solution.py
+++ b/solution.py
@@ -13,6 +13,7 @@
 MESH = pl.DeviceIdType.MESH
 HIGH = lax.Precision.HIGHEST
 LANES = 128
+SUPER = 64
 
 
 def blocks_of(bands):
@@ -269,75 +270,88 @@
                 m[b * LANES:b * LANES + size, q * LANES:(q + 1) * LANES] = block[:size]
     sub = lax.broadcasted_iota(jnp.int32, (8, LANES), 0)
     lane = lax.broadcasted_iota(jnp.int32, (8, LANES), 1)
+    tiles = wide // LANES
+
+    def superblock(start):
+        size = min(SUPER, bands - start)
+        count = size // 8
+        panels = [[m[start + 8 * i:start + 8 * i + 8, t * LANES:(t + 1) * LANES] for t in range(tiles)]
+                  for i in range(count)]
+        done = []
+        for k in range(count):
+            top = start + 8 * k
+            at, lane0 = top // LANES, top % LANES
+            own = panels[k]
+            cols = [jnp.broadcast_to(own[at][:, lane0 + e:lane0 + e + 1], (8, LANES)) for e in range(8)]
+            later = range(k + 1, count)
+            below = {p: [jnp.broadcast_to(panels[p][at][:, lane0 + e:lane0 + e + 1], (8, LANES)) for e in range(8)]
+                     for p in later}
+            inside = (lane >= lane0) & (lane < lane0 + 8)
+            own[at] = jnp.where(inside, jnp.where(lane - lane0 == sub, 1.0, 0.0), own[at])
+            for p in later:
+                panels[p][at] = jnp.where(inside, 0.0, panels[p][at])
+            pivots = None
+            for b in range(8):
+                pivot = jnp.broadcast_to(cols[b][b:b + 1, :], (8, LANES))
+                inverse = 1.0 / pivot
+                pivots = pivot if pivots is None else jnp.where(sub == b, pivot, pivots)
+                factor = jnp.where(sub > b, cols[b] * inverse, 0.0)
+                rows_b = [jnp.broadcast_to(own[t][b:b + 1, :], (8, LANES)) for t in range(tiles)]
+                heads = {e: jnp.broadcast_to(cols[e][b:b + 1, :], (8, LANES)) for e in range(b + 1, 8)}
+                for e in range(b + 1, 8):
+                    cols[e] = cols[e] - factor * heads[e]
+                for p in later:
+                    scaled = below[p][b] * inverse
+                    for e in range(b + 1, 8):
+                        below[p][e] = below[p][e] - scaled * heads[e]
+                    for t in range(tiles):
+                        panels[p][t] = panels[p][t] - scaled * rows_b[t]
+                if b < 7:
+                    for t in range(tiles):
+                        own[t] = own[t] - factor * rows_b[t]
+            root = lax.rsqrt(pivots)
+            done.append([own[t] * root for t in range(tiles)])
+            for t in range(tiles):
+                m[top:top + 8, t * LANES:(t + 1) * LANES] = done[k][t]
+        below_at = start + size
+        if below_at >= bands:
+            return
+        full = [jnp.concatenate([done[k][t] for k in range(count)], axis=0) for t in range(tiles)]
+        kept = list(full)
+        row_ids = lax.broadcasted_iota(jnp.int32, (size, LANES), 0) + start % LANES
+        lane_ids = lax.broadcasted_iota(jnp.int32, (size, LANES), 1)
+        upper = (lane_ids > row_ids) & (lane_ids < start % LANES + size)
+        kept[start // LANES] = jnp.where(upper, 0.0, kept[start // LANES])
+        splits = [split3(part) for part in kept]
+        right = jnp.concatenate(
+            [jnp.concatenate([splits[t][0], splits[t][0], splits[t][0], splits[t][1], splits[t][2], splits[t][1]], axis=0)
+             for t in range(tiles)], axis=1).astype(jnp.bfloat16)
+        half_lanes = lax.broadcasted_iota(jnp.int32, (LANES, LANES), 1) < size
+        for t in range(below_at // LANES, tiles):
+            flipped = jnp.transpose(jnp.concatenate([full[t], full[t]], axis=0))
+            one, two, three = split3(flipped)
+            first_pair = jnp.where(half_lanes, one, two)
+            second_pair = jnp.where(half_lanes, three, one)
+            left = jnp.concatenate([first_pair, second_pair, first_pair], axis=1).astype(jnp.bfloat16)
+            lo = max(below_at, t * LANES)
+            bounds = [lo]
+            while bounds[-1] < min(bands, (t + 1) * LANES):
+                bounds.append(min(bounds[-1] + SUPER, bands, (t + 1) * LANES))
+            for low_row, high_row in zip(bounds[:-1], bounds[1:]):
+                update = lax.dot_general(
+                    left[low_row - t * LANES:high_row - t * LANES], right, (((1,), (0,)), ((), ())),
+                    preferred_element_type=jnp.float32)
+                for u in range(tiles):
+                    old = m[low_row:high_row, u * LANES:(u + 1) * LANES]
+                    if start // LANES == u:
+                        lanes = lax.broadcasted_iota(jnp.int32, (high_row - low_row, LANES), 1)
+                        old = jnp.where((lanes >= start % LANES) & (lanes < start % LANES + size), 0.0, old)
+                    m[low_row:high_row, u * LANES:(u + 1) * LANES] = old - update[:, u * LANES:(u + 1) * LANES]
 
     def eliminate(c):
-        top = c * LANES
-        span = bands - top
-
-        def step(j, carry):
-            row = pl.multiple_of(top + 8 * j, 8)
-            here = m[pl.ds(row, 8), top:top + LANES]
-            small = pltpu.roll(here, lax.rem(LANES - 8 * j, LANES), 1)
-            columns = [jnp.broadcast_to(small[:, b:b + 1], (8, LANES)) for b in range(8)]
-            d = [[jnp.broadcast_to(columns[b][a:a + 1, :], (8, LANES)) if b <= a else None
-                  for b in range(8)] for a in range(8)]
-            low = [[None] * 8 for _ in range(8)]
-            root = [None] * 8
-            for b in range(8):
-                root[b] = lax.rsqrt(d[b][b])
-                for a in range(b + 1, 8):
-                    low[a][b] = d[a][b] * root[b]
-                for a in range(b + 1, 8):
-                    for e in range(b + 1, a + 1):
-                        d[a][e] = d[a][e] - low[a][b] * low[e][b]
-            inv = [[None] * 8 for _ in range(8)]
-            for b in range(8):
-                inv[b][b] = root[b]
-                for a in range(b + 1, 8):
-                    acc = low[a][b] * inv[b][b]
-                    for e in range(b + 1, a):
-                        acc = acc + low[a][e] * inv[e][b]
-                    inv[a][b] = -(acc * root[a])
-            wcol = []
-            for b in range(8):
-                col = jnp.where(sub == b, inv[b][b], 0.0)
-                for a in range(b + 1, 8):
-                    col = jnp.where(sub == a, inv[a][b], col)
-                wcol.append(col)
-            tiles = []
-            for t in range(wide // LANES):
-                acc = None
-                panel = m[pl.ds(row, 8), t * LANES:(t + 1) * LANES]
-                for b in range(8):
-                    term = wcol[b] * panel[b:b + 1, :]
-                    acc = term if acc is None else acc + term
-                if t == c:
-                    for b in range(8):
-                        acc = jnp.where(lane == 8 * j + b, wcol[b], acc)
-                tiles.append(acc)
-            r = jnp.concatenate(tiles, axis=1)
-            m[pl.ds(row, 8), :] = r
-            one, two, three = split3(r)
-            right = jnp.concatenate([one, two, three, one, two, one], axis=0)
-            cols = lax.broadcasted_iota(jnp.int32, (8, wide), 1)
-            keep = (cols >= row + 8).astype(jnp.float32)
-            l1, l2, l3 = one * keep, two * keep, three * keep
-            left = jnp.concatenate([l1, l1, l1, l2, l2, l3], axis=0)[:, top:]
-            update = lax.dot_general(
-                left.astype(jnp.bfloat16), right.astype(jnp.bfloat16),
-                (((0,), (0,)), ((), ())), preferred_element_type=jnp.float32)
-            for t in range(wide // LANES):
-                part = slice(t * LANES, (t + 1) * LANES)
-                old = m[top:bands, part]
-                if t == c:
-                    line_ids = lax.broadcasted_iota(jnp.int32, (span, LANES), 0)
-                    lane_ids = lax.broadcasted_iota(jnp.int32, (span, LANES), 1)
-                    inside = (lane_ids >= 8 * j) & (lane_ids < 8 * j + 8) & (line_ids >= 8 * j + 8)
-                    old = jnp.where(inside, 0.0, old)
-                m[top:bands, part] = old - update[:span, part]
-            return carry
-
-        lax.fori_loop(0, min(LANES, span) // 8, step, 0)
+        for start in range(c * LANES, min(bands, (c + 1) * LANES), SUPER):
+            superblock(start)
+
     eliminate(0)
     rim_wait(pair)
     h, w = lines // 2, width // 2

time: 66.3 us -> 53.5 us (0.81)
  Pallas kernels: 61.2 us -> 48.4 us
    pallas_call x1, Pallas kernels: 61.2 us -> 48.4 us  [gram_call(): pl.pallas_call(functools.partial(gram_kernel, samp, line, bands, lines, w...]
where the time goes in v1:
time: 53.5 us; the launch traced here: 53.2 us
  Pallas kernels  48.4 us (90%)
  local copies, waits for them, and re-layouts  4.12 us (8%)
  between operations  0.65 us (1%)
    pallas_call x1, Pallas kernels, gram_call(): pl.pallas_call(functools.partial(gram_kernel, samp, line, bands, lines, w...  48.4 us
    unnamed x10, local copies, waits for them, and re-layouts  4.12 us

profile of v1, /device:TPU:0, one launch (start us, length us, event | category | flops | bytes accessed | tf_op | source)
XLA Modules:
  0.0 53.2 jit_solution(6806026146000874292)
XLA Ops:
  0.6 48.4 %shard_map.46 = (f32[3,432,128]{2,1,0:T(8,128)}, f32[324,128]{1,0:T(8,128)}, f32[81,128]{1,0:T(8,128)}, f32[27,128]{1,0:T(8,128)}) custom-call(f32[1728,128]{1,0:T(8,128)} %bitcast.5), custom_call_target="tpu_custom_call" | custom-call | tf_op jit(solution)/shard_map/pallas_call | solution.py:419
  49.1 0.0 copy-start
  49.1 2.0 %copy.9 = f32[165888]{0:T(1024)} copy(f32[165888]{0:T(1024)} %bitcast.6) | data formatting | bytes 1327104
  51.1 0.0 copy-done
  51.1 0.0 copy-start.1
  51.1 0.7 %copy.10 = f32[41472]{0:T(1024)} copy(f32[41472]{0:T(1024)S(1)} %bitcast.7) | data formatting | bytes 331776
  51.8 0.1 copy-done.1
  51.9 0.0 copy-start.2
  51.9 0.6 %copy.11 = f32[10368]{0:T(1024)} copy(f32[10368]{0:T(1024)S(1)} %bitcast.8) | data formatting | bytes 82944
  52.5 0.1 copy-done.2
  52.6 0.6 %copy.12 = f32[3456]{0:T(1024)} copy(f32[3456]{0:T(1024)S(1)} %bitcast.9) | data formatting | bytes 27648
Async XLA Ops:
  49.1 2.0 %copy-start = (f32[324,128]{1,0:T(8,128)S(1)}, f32[324,128]{1,0:T(8,128)}, u32[]{:S(2)}) copy-start(f32[324,128]{1,0:T(8,128)} %get-tuple-element.9) | copy-start | bytes 497668
  51.1 0.8 %copy-start.1 = (f32[81,128]{1,0:T(8,128)S(1)}, f32[81,128]{1,0:T(8,128)}, u32[]{:S(2)}) copy-start(f32[81,128]{1,0:T(8,128)} %get-tuple-element.10) | copy-start | bytes 124420
  51.9 0.7 %copy-start.2 = (f32[27,128]{1,0:T(8,128)S(1)}, f32[27,128]{1,0:T(8,128)}, u32[]{:S(2)}) copy-start(f32[27,128]{1,0:T(8,128)} %get-tuple-element.11) | copy-start | bytes 41476

commit v2 on v1

--- a/solution.py
+++ b/solution.py
@@ -89,7 +89,7 @@
     return first, second, rest - second
 
 
-def gram_kernel(samp, line, bands, lines, width, x_ref, o1_ref, o2_ref, o3_ref, o4_ref, t_ref, m, rest, corr, v1, v2, v3, z1, z2, z3, n1, n2, n3, el1, er1, el2, er2, el3, er3, fl1, fr1, fl2, fr2, fl3, fr3,
+def gram_kernel(samp, line, bands, lines, width, x_ref, o1_ref, o2_ref, o3_ref, o4_ref, t_ref, th, tl, m, rest, corr, v1, v2, v3, z1, z2, z3, n1, n2, n3, el1, er1, el2, er2, el3, er3, fl1, fr1, fl2, fr2, fl3, fr3,
                 l_send, l_recv, r_send, r_recv, xs, sums, sums_in, g, half_in,
                 chunk_in, tot, s_send, s_recv, h_send, h_recv, c_send, c_recv, a_send, a_recv,
                 b_send, b_recv):
@@ -149,10 +149,19 @@
         pl.semaphore_signal(barrier, inc=1, device_id=peer(d), device_id_type=MESH)
     if padded > bands:
         xs[bands:, :] = jnp.zeros((padded - bands, pixels), jnp.float32)
+    parts = [x_ref[pl.ds(q, bands, stride=packs), :] for q in range(packs)]
+    folded = parts[0]
+    for part in parts[1:]:
+        folded = folded + part
+    if padded > bands:
+        folded = jnp.concatenate([folded, jnp.zeros((padded - bands, LANES), jnp.float32)], axis=0)
+    folded = jnp.concatenate(split3(folded), axis=1).astype(jnp.bfloat16)
+    sums[...] = lax.dot_general(jnp.ones((8, 3 * LANES), jnp.bfloat16), folded, (((1,), (1,)), ((), ())),
+                                preferred_element_type=jnp.float32)[0:1]
+    centre = lax.dot_general(folded[0:bands], jnp.ones((3 * LANES, LANES), jnp.bfloat16), (((1,), (0,)), ((), ())),
+                             preferred_element_type=jnp.float32) / float(pixels)
     for q in range(packs):
-        xs[0:bands, q * LANES:(q + 1) * LANES] = x_ref[pl.ds(q, bands, stride=packs), :]
-    sums[...] = lax.dot_general(jnp.ones((8, pixels), jnp.float32), xs[...], (((1,), (1,)), ((), ())),
-                                precision=HIGH, preferred_element_type=jnp.float32)[0:1]
+        xs[0:bands, q * LANES:(q + 1) * LANES] = parts[q] - centre
     pl.semaphore_wait(barrier, devices - 1)
     copies = []
     for d in range(1, devices):
@@ -162,12 +171,17 @@
         copies.append(copy)
     sum_copies = copies
     local_mean = sums[...] / float(pixels)
-    xs[...] = xs[...] - jnp.transpose(jnp.broadcast_to(local_mean, (8, padded)))[:, 0:1]
     rows, offsets = blocks_of(bands)
-    for q, (count, offset) in enumerate(zip(rows, offsets)):
-        g[offset:offset + count, :] = lax.dot_general(
-            xs[q * LANES:q * LANES + count, :], xs[q * LANES:(q + 1) * LANES, :],
-            (((1,), (1,)), ((), ())), precision=HIGH, preferred_element_type=jnp.float32)
+    coarse = xs[...].astype(jnp.bfloat16)
+    fine = (xs[...] - coarse.astype(jnp.float32)).astype(jnp.bfloat16)
+    tall = jnp.concatenate([coarse, coarse, fine, fine], axis=1)
+    flat_right = jnp.concatenate([coarse, fine, coarse, fine], axis=1)
+    for q in range(0, len(rows), 2):
+        span = min(2 * LANES, padded - q * LANES)
+        both = lax.dot_general(tall[q * LANES:bands], flat_right[q * LANES:q * LANES + span],
+                               (((1,), (1,)), ((), ())), preferred_element_type=jnp.float32)
+        for b in range(span // LANES):
+            g[offsets[q + b]:offsets[q + b] + rows[q + b], :] = both[b * LANES:, b * LANES:(b + 1) * LANES]
     used = offsets[-1] + rows[-1]
     if g.shape[0] > used:
         g[used:, :] = jnp.zeros((g.shape[0] - used, LANES), jnp.float32)
@@ -278,11 +292,18 @@
         panels = [[m[start + 8 * i:start + 8 * i + 8, t * LANES:(t + 1) * LANES] for t in range(tiles)]
                   for i in range(count)]
         done = []
+
+        def spread(tile, lane0):
+            return [jnp.broadcast_to(tile[:, lane0 + e:lane0 + e + 1], (8, LANES)) for e in range(8)]
+
+        ahead = spread(panels[0][start // LANES], start % LANES)
         for k in range(count):
             top = start + 8 * k
             at, lane0 = top // LANES, top % LANES
             own = panels[k]
-            cols = [jnp.broadcast_to(own[at][:, lane0 + e:lane0 + e + 1], (8, LANES)) for e in range(8)]
+            cols = ahead
+            if k + 1 < count:
+                ahead = spread(panels[k + 1][(top + 8) // LANES], (top + 8) % LANES)
             later = range(k + 1, count)
             below = {p: [jnp.broadcast_to(panels[p][at][:, lane0 + e:lane0 + e + 1], (8, LANES)) for e in range(8)]
                      for p in later}
@@ -302,6 +323,9 @@
                     cols[e] = cols[e] - factor * heads[e]
                 for p in later:
                     scaled = below[p][b] * inverse
+                    if p == k + 1:
+                        ahead = [ahead[e] - scaled * jnp.broadcast_to(below[p][b][e:e + 1, :], (8, LANES))
+                                 for e in range(8)]
                     for e in range(b + 1, 8):
                         below[p][e] = below[p][e] - scaled * heads[e]
                     for t in range(tiles):
@@ -323,16 +347,24 @@
         upper = (lane_ids > row_ids) & (lane_ids < start % LANES + size)
         kept[start // LANES] = jnp.where(upper, 0.0, kept[start // LANES])
         splits = [split3(part) for part in kept]
+        terms = ((0, 0), (1, 0), (2, 0), (0, 1), (0, 2), (1, 1))
+        copies = LANES // size
+        depth = -(-len(terms) // copies)
+        zero = jnp.zeros((size, LANES), jnp.float32)
         right = jnp.concatenate(
-            [jnp.concatenate([splits[t][0], splits[t][0], splits[t][0], splits[t][1], splits[t][2], splits[t][1]], axis=0)
+            [jnp.concatenate([splits[t][b] for a, b in terms] + [zero] * (depth * copies - len(terms)), axis=0)
              for t in range(tiles)], axis=1).astype(jnp.bfloat16)
-        half_lanes = lax.broadcasted_iota(jnp.int32, (LANES, LANES), 1) < size
+        which = lax.broadcasted_iota(jnp.int32, (LANES, LANES), 1) // size
         for t in range(below_at // LANES, tiles):
-            flipped = jnp.transpose(jnp.concatenate([full[t], full[t]], axis=0))
-            one, two, three = split3(flipped)
-            first_pair = jnp.where(half_lanes, one, two)
-            second_pair = jnp.where(half_lanes, three, one)
-            left = jnp.concatenate([first_pair, second_pair, first_pair], axis=1).astype(jnp.bfloat16)
+            flipped = split3(jnp.transpose(jnp.concatenate([full[t]] * copies, axis=0)))
+            pieces = []
+            for g in range(depth):
+                group = [flipped[a] for a, b in terms[g * copies:(g + 1) * copies]]
+                piece = group[0]
+                for i in range(1, copies):
+                    piece = jnp.where(which == i, group[i] if i < len(group) else 0.0, piece)
+                pieces.append(piece)
+            left = jnp.concatenate(pieces, axis=1).astype(jnp.bfloat16)
             lo = max(below_at, t * LANES)
             bounds = [lo]
             while bounds[-1] < min(bands, (t + 1) * LANES):
@@ -348,61 +380,110 @@
                         old = jnp.where((lanes >= start % LANES) & (lanes < start % LANES + size), 0.0, old)
                     m[low_row:high_row, u * LANES:(u + 1) * LANES] = old - update[:, u * LANES:(u + 1) * LANES]
 
-    def eliminate(c):
-        for start in range(c * LANES, min(bands, (c + 1) * LANES), SUPER):
-            superblock(start)
-
-    eliminate(0)
-    rim_wait(pair)
     h, w = lines // 2, width // 2
     one = h * w
-    lift_samples(z1, fl1, fr1, lines, width, first, last, ((v2, 0), (t_ref, 0), (t_ref, one), (t_ref, 2 * one)))
-    lines2 = line_copy(1, v2, n2, h, w)
-    eliminate(1)
-    lines2.wait()
-    lift_lines(v2, n2, z2, h, w, ln)
-    rims(z2, h, w, el2, er2)
-    pair2 = rim_copies(1, el2, er2, fl2, fr2)
-    eliminate(2)
-    rim_wait(pair2)
-    two, base2 = one // 4, 3 * one
-    lift_samples(z2, fl2, fr2, h, w, first, last,
-                 ((v3, 0), (t_ref, base2), (t_ref, base2 + two), (t_ref, base2 + 2 * two)))
-    h, w = h // 2, w // 2
-    lines3 = line_copy(2, v3, n3, h, w)
-    lines3.wait()
-    lift_lines(v3, n3, z3, h, w, ln)
-    rims(z3, h, w, el3, er3)
-    pair3 = rim_copies(2, el3, er3, fl3, fr3)
-    for c in range(3, len(rows)):
-        eliminate(c)
-    rim_wait(pair3)
-    three, base3 = two // 4, base2 + 3 * two
-    lift_samples(z3, fl3, fr3, h, w, first, last,
-                 ((t_ref, base3 + 3 * three), (t_ref, base3), (t_ref, base3 + three), (t_ref, base3 + 2 * three)))
-    keep = lax.broadcasted_iota(jnp.int32, (bands, wide), 1) <= lax.broadcasted_iota(
-        jnp.int32, (bands, wide), 0)
-    m[...] = jnp.where(keep, m[...], 0.0)
-    for q in range(t_ref.shape[1] // LANES):
-        part = jnp.concatenate([t_ref[t, q * LANES:(q + 1) * LANES, :] for t in range(wide // LANES)], axis=1)
-        out = lax.dot_general(m[...], part, (((1,), (1,)), ((), ())),
-                              precision=HIGH, preferred_element_type=jnp.float32)
-        if q < o1_ref.shape[0]:
-            o1_ref[q] = out
-        else:
-            rest[...] = out
-
-
-    def pack(dest, at, lane0, wide_out):
+    two = one // 4
+    three = two // 4
+    base2, base3 = 3 * one, 3 * one + 3 * two
+    state = {}
+
+    def stage0():
+        rim_wait(pair)
+        lift_samples(z1, fl1, fr1, lines, width, first, last, ((v2, 0), (t_ref, 0), (t_ref, one), (t_ref, 2 * one)))
+        state["lines"] = line_copy(1, v2, n2, h, w)
+
+    def stage1():
+        state["lines"].wait()
+        lift_lines(v2, n2, z2, h, w, ln)
+        rims(z2, h, w, el2, er2)
+        state["pair"] = rim_copies(1, el2, er2, fl2, fr2)
+
+    def stage2():
+        rim_wait(state["pair"])
+        lift_samples(z2, fl2, fr2, h, w, first, last,
+                     ((v3, 0), (t_ref, base2), (t_ref, base2 + two), (t_ref, base2 + 2 * two)))
+        state["lines"] = line_copy(2, v3, n3, h // 2, w // 2)
+
+    def stage3():
+        state["lines"].wait()
+        lift_lines(v3, n3, z3, h // 2, w // 2, ln)
+        rims(z3, h // 2, w // 2, el3, er3)
+        state["pair"] = rim_copies(2, el3, er3, fl3, fr3)
+
+    def stage4():
+        rim_wait(state["pair"])
+        lift_samples(z3, fl3, fr3, h // 2, w // 2, first, last,
+                     ((t_ref, base3 + 3 * three), (t_ref, base3), (t_ref, base3 + three), (t_ref, base3 + 2 * three)))
+        for t in range(tiles):
+            top_part = t_ref[t].astype(jnp.bfloat16)
+            th[t] = top_part
+            tl[t] = (t_ref[t] - top_part.astype(jnp.float32)).astype(jnp.bfloat16)
+
+    def pack(dest, at, lane0, wide_out, low_row, count):
         group = LANES // wide_out
-        count = bands // group
-        pieces = [rest[pl.ds(b, count, stride=group), :][:, lane0:lane0 + wide_out] for b in range(group)]
-        dest[at:at + count, :] = jnp.concatenate(pieces, axis=1)
-
-    for i in range(3):
-        pack(o2_ref, i * (o2_ref.shape[0] // 3), i * two, two)
-        pack(o3_ref, i * (o3_ref.shape[0] // 3), 3 * two + i * three, three)
-    pack(o4_ref, 0, 3 * two + 3 * three, three)
+        pieces = [rest[pl.ds(low_row + b, count // group, stride=group), :][:, lane0:lane0 + wide_out]
+                  for b in range(group)]
+        at = at + low_row // group
+        dest[at:at + count // group, :] = jnp.concatenate(pieces, axis=1)
+
+    def final(r):
+        low_row = r * LANES
+        count = min(LANES, bands - low_row)
+        keep = lax.broadcasted_iota(jnp.int32, (count, LANES), 1) <= lax.broadcasted_iota(jnp.int32, (count, LANES), 0)
+        parts = [m[low_row:low_row + count, t * LANES:(t + 1) * LANES] for t in range(r + 1)]
+        parts[r] = jnp.where(keep, parts[r], 0.0)
+        whole = jnp.concatenate(parts, axis=1)
+        upper = whole.astype(jnp.bfloat16)
+        lower = (whole - upper.astype(jnp.float32)).astype(jnp.bfloat16)
+        left = jnp.concatenate([upper, lower, upper], axis=1)
+        chunks = t_ref.shape[1] // LANES
+        for q in range(0, chunks, 2):
+            pix = slice(q * LANES, min(q + 2, chunks) * LANES)
+            big = [th[t, pix, :] for t in range(r + 1)]
+            small = [tl[t, pix, :] for t in range(r + 1)]
+            right = jnp.concatenate(big + big + small, axis=1)
+            out = lax.dot_general(left, right, (((1,), (1,)), ((), ())), preferred_element_type=jnp.float32)
+            for b in range(out.shape[1] // LANES):
+                part = out[:, b * LANES:(b + 1) * LANES]
+                if q + b < o1_ref.shape[0]:
+                    o1_ref[q + b, low_row:low_row + count, :] = part
+                else:
+                    rest[low_row:low_row + count, :] = part
+        for i in range(3):
+            pack(o2_ref, i * (o2_ref.shape[0] // 3), i * two, two, low_row, count)
+            pack(o3_ref, i * (o3_ref.shape[0] // 3), 3 * two + i * three, three, low_row, count)
+        pack(o4_ref, 0, 3 * two + 3 * three, three, low_row, count)
+
+    stages = [stage0, stage1, stage2, stage3, stage4]
+    ready = 0
+    for start in range(0, bands, SUPER):
+        superblock(start)
+        if stages:
+            stages.pop(0)()
+        if not stages:
+            while ready * LANES < bands and min(bands, (ready + 1) * LANES) <= start + SUPER:
+                final(ready)
+                ready += 1
+
+
+def store_kernel(*refs):
+    count = len(refs) // 2
+    copies = [pltpu.make_async_copy(refs[i], refs[count + i], refs[-1].at[i]) for i in range(count)]
+    for copy in copies:
+        copy.start()
+    for copy in copies:
+        copy.wait()
+
+
+def store_call(arrays):
+    return pl.pallas_call(
+        store_kernel,
+        out_shape=tuple(jax.ShapeDtypeStruct(a.shape, a.dtype) for a in arrays),
+        in_specs=[pl.BlockSpec(memory_space=pltpu.VMEM)] * len(arrays),
+        out_specs=(pl.BlockSpec(memory_space=pl.ANY),) * len(arrays),
+        scratch_shapes=[pltpu.SemaphoreType.DMA((len(arrays),))],
+        compiler_params=pltpu.CompilerParams(vmem_limit_bytes=4 * 1024 * 1024),
+    )(*arrays)
 
 
 def gram_call(cube, bands, lines, width):
@@ -425,7 +506,9 @@
         in_specs=[pl.BlockSpec(memory_space=pltpu.VMEM)],
         out_specs=(pl.BlockSpec(memory_space=pltpu.VMEM),) * 4,
         scratch_shapes=[
-            pltpu.VMEM((padded // LANES, pixels, LANES), f32), pltpu.VMEM((bands, padded), f32),
+            pltpu.VMEM((padded // LANES, pixels, LANES), f32),
+            pltpu.VMEM((padded // LANES, pixels, LANES), jnp.bfloat16),
+            pltpu.VMEM((padded // LANES, pixels, LANES), jnp.bfloat16), pltpu.VMEM((bands, padded), f32),
             pltpu.VMEM((bands, LANES), f32), pltpu.VMEM((total, LANES), f32),
             *[pltpu.VMEM((padded // LANES, pixels // 4 ** i, LANES), f32) for i in (0, 1, 2)],
             *[pltpu.VMEM((padded // LANES, pixels // 4 ** i, LANES), f32) for i in (0, 1, 2)],
@@ -441,12 +524,13 @@
             sem((samp - 1,)), sem((samp - 1,)), sem((samp - 1,)), sem((samp - 1,)),
             sem((line - 1,)), sem((line - 1,)),
         ],
-        compiler_params=pltpu.CompilerParams(collective_id=0, has_side_effects=True),
+        compiler_params=pltpu.CompilerParams(collective_id=0, has_side_effects=True,
+                                             vmem_limit_bytes=32 * 1024 * 1024),
     )(cube.reshape(-1, LANES))
 
 
 def local(cube):
-    return tuple(out.reshape(-1) for out in gram_call(cube, BANDS, LD, SD))
+    return tuple(out.reshape(-1) for out in store_call(gram_call(cube, BANDS, LD, SD)))
 
 
 def solution(mesh):

time: 53.5 us -> 44.2 us (0.83)
  Pallas kernels: 48.4 us -> 42.2 us
  local copies, waits for them, and re-layouts: 4.12 us -> 1.16 us
    pallas_call x1, Pallas kernels: 48.4 us -> 41.3 us  [gram_call(): pl.pallas_call(functools.partial(gram_kernel, samp, line, bands, lines, w...]
    unnamed x10 -> x2, local copies, waits for them, and re-layouts: 4.12 us -> 1.16 us
    pallas_call x0 -> x1, Pallas kernels: none -> 0.93 us  [store_call(): pl.pallas_call(store_kernel, out_shape=tuple((jax.ShapeDtypeStruct(a.shap...]
where the time goes in v2:
time: 44.2 us; the launch traced here: 44 us
  Pallas kernels  42.2 us (95%)
  local copies, waits for them, and re-layouts  1.16 us (3%)
  between operations  0.65 us (1%)
    pallas_call x1, Pallas kernels, gram_call(): pl.pallas_call(functools.partial(gram_kernel, samp, line, bands, lines, w...  41.3 us
    unnamed x2, local copies, waits for them, and re-layouts  1.16 us
    pallas_call x1, Pallas kernels, store_call(): pl.pallas_call(store_kernel, out_shape=tuple((jax.ShapeDtypeStruct(a.shap...  0.93 us

profile of v2, /device:TPU:0, one launch (start us, length us, event | category | flops | bytes accessed | tf_op | source)
XLA Modules:
  0.0 44.0 jit_solution(6806950480623622732)
XLA Ops:
  0.6 0.0 copy-start
  0.6 1.2 %copy-done = f32[221184]{0:T(1024)S(1)} copy-done((f32[221184]{0:T(1024)S(1)}, f32[221184]{0:T(1024)}, u32[]{:S(2)}) %copy-start) | copy-done | bytes 884760
  1.8 41.3 %shard_map.46 = (f32[3,432,128]{2,1,0:T(8,128)S(1)}, f32[324,128]{1,0:T(8,128)S(1)}, f32[81,128]{1,0:T(8,128)S(1)}, f32[27,128]{1,0:T(8,128)S(1)}) custom-call(f32[1728,128]{1,0:T(8,128)S(1)} %bitcast.5), custom_call_target="tpu_custom_call" | custom-call | tf_op jit(solution)/shard_map/pallas_call | solution.py:500
  43.1 0.9 %shard_map.47 = (f32[3,432,128]{2,1,0:T(8,128)}, f32[324,128]{1,0:T(8,128)}, f32[81,128]{1,0:T(8,128)}, f32[27,128]{1,0:T(8,128)}) custom-call(f32[3,432,128]{2,1,0:T(8,128)S(1)} %get-tuple-element.12.refs_0_, f32[324,128]{1,0:T(8,128)S(1)} %get-tuple-element.13.refs_1_, f32[81,128]{1,0:T(8,128)S(1)} %get-tuple-element.14.refs_2_, ...), custom_call_target="tpu_custom_call" | custom-call | tf_op jit(solution)/shard_map/pallas_call | solution.py:479
Async XLA Ops:
  0.6 1.2 %copy-start = (f32[221184]{0:T(1024)S(1)}, f32[221184]{0:T(1024)}, u32[]{:S(2)}) copy-start(f32[221184]{0:T(1024)} %param.1) | copy-start | bytes 2654212

commit v3 on v2

--- a/solution.py
+++ b/solution.py
@@ -39,11 +39,15 @@
     return [e * (1.0 / scale_lift) for e in evens], [o * scale_lift for o in odds[1:]]
 
 
-def lift_lines(src, halo, dst, lines, width, ln):
+def lift_lines(src, halo, dst, lines, width, ln, centre=None):
     half = lines // 2
     for t in range(src.shape[0]):
         own = [src[t, i * width:(i + 1) * width] for i in range(lines)]
         got = [halo[t, i * width:(i + 1) * width] for i in range(RIM)]
+        if centre is not None:
+            middle = centre[:, t * LANES:(t + 1) * LANES]
+            own = [o - middle for o in own]
+            got = [o - middle for o in got]
         before = [jnp.where(ln == 0, own[RIM - i], got[i]) for i in range(RIM)]
         after = [jnp.where(ln == 0, got[i], own[lines - 2 - i]) for i in range(RIM)]
         low, high = lift_list(before + own + after)
@@ -147,22 +151,32 @@
     barrier = pltpu.get_barrier_semaphore()
     for d in range(1, devices):
         pl.semaphore_signal(barrier, inc=1, device_id=peer(d), device_id_type=MESH)
-    if padded > bands:
-        xs[bands:, :] = jnp.zeros((padded - bands, pixels), jnp.float32)
-    parts = [x_ref[pl.ds(q, bands, stride=packs), :] for q in range(packs)]
-    folded = parts[0]
+    rows, offsets = blocks_of(bands)
+    used = offsets[-1] + rows[-1]
+    for q in range(packs):
+        part = x_ref[pl.ds(q, bands, stride=packs), :]
+        xs[0:bands, q * LANES:(q + 1) * LANES] = part
+        if padded > bands:
+            xs[bands:, q * LANES:(q + 1) * LANES] = jnp.zeros((padded - bands, LANES), jnp.float32)
+    for t in range(v1.shape[0]):
+        v1[t] = jnp.transpose(xs[t * LANES:(t + 1) * LANES, :])
+    folded = xs[:, 0:LANES]
+    for q in range(1, packs):
+        folded = folded + xs[:, q * LANES:(q + 1) * LANES]
+    folded = jnp.concatenate(split3(folded), axis=1).astype(jnp.bfloat16)
+    row_sums = lax.dot_general(jnp.ones((8, 3 * LANES), jnp.bfloat16), folded, (((1,), (1,)), ((), ())),
+                               preferred_element_type=jnp.float32)[0:1]
+    centre = lax.dot_general(folded, jnp.ones((3 * LANES, LANES), jnp.bfloat16), (((1,), (0,)), ((), ())),
+                             preferred_element_type=jnp.float32) / float(pixels)
+    parts = [xs[:, q * LANES:(q + 1) * LANES] - centre for q in range(packs)]
+    energy = parts[0] * parts[0]
     for part in parts[1:]:
-        folded = folded + part
-    if padded > bands:
-        folded = jnp.concatenate([folded, jnp.zeros((padded - bands, LANES), jnp.float32)], axis=0)
-    folded = jnp.concatenate(split3(folded), axis=1).astype(jnp.bfloat16)
-    sums[...] = lax.dot_general(jnp.ones((8, 3 * LANES), jnp.bfloat16), folded, (((1,), (1,)), ((), ())),
-                                preferred_element_type=jnp.float32)[0:1]
-    centre = lax.dot_general(folded[0:bands], jnp.ones((3 * LANES, LANES), jnp.bfloat16), (((1,), (0,)), ((), ())),
-                             preferred_element_type=jnp.float32) / float(pixels)
-    for q in range(packs):
-        xs[0:bands, q * LANES:(q + 1) * LANES] = parts[q] - centre
+        energy = energy + part * part
+    energy = jnp.sum(jnp.sum(energy, axis=0, keepdims=True), axis=1, keepdims=True)
+    sum_lane = lax.broadcasted_iota(jnp.int32, (1, padded), 1)
+    sums[...] = jnp.where(sum_lane < bands, row_sums, energy)
     pl.semaphore_wait(barrier, devices - 1)
+    lines1 = line_copy(0, v1, n1, lines, width)
     copies = []
     for d in range(1, devices):
         copy = pltpu.make_async_remote_copy(sums, sums_in.at[d - 1], s_send.at[d - 1], s_recv.at[d - 1],
@@ -170,118 +184,168 @@
         copy.start()
         copies.append(copy)
     sum_copies = copies
-    local_mean = sums[...] / float(pixels)
-    rows, offsets = blocks_of(bands)
-    coarse = xs[...].astype(jnp.bfloat16)
-    fine = (xs[...] - coarse.astype(jnp.float32)).astype(jnp.bfloat16)
-    tall = jnp.concatenate([coarse, coarse, fine, fine], axis=1)
-    flat_right = jnp.concatenate([coarse, fine, coarse, fine], axis=1)
+    local_mean = row_sums / float(pixels)
+    coarse = [part.astype(jnp.bfloat16) for part in parts]
+    fine = [(part - top_part.astype(jnp.float32)).astype(jnp.bfloat16) for part, top_part in zip(parts, coarse)]
+    tall = jnp.concatenate(coarse + coarse + fine + fine, axis=1)
+    flat_right = jnp.concatenate(coarse + fine + coarse + fine, axis=1)
+    part_rows = g.shape[0] // 2
+    half = part_rows // line
+    chunk = half // samp
+
+    def line_swap(p):
+        made = []
+        for d in range(1, line):
+            other = lax.rem(ln + d, line)
+            copy = pltpu.make_async_remote_copy(
+                g.at[pl.ds(pl.multiple_of(p * part_rows + other * half, 8), half)], half_in.at[p, d - 1],
+                h_send.at[p, d - 1], h_recv.at[p, d - 1], device_id={"line": other}, device_id_type=MESH)
+            copy.start()
+            made.append(copy)
+        return made
+
+    def scatter(p, swaps):
+        for copy in swaps:
+            copy.wait()
+        mine = pl.ds(pl.multiple_of(p * part_rows + ln * half, 8), half)
+        value = g[mine, :]
+        for d in range(1, line):
+            value = value + half_in[p, d - 1]
+        g[mine, :] = value
+        made = []
+        for d in range(1, samp):
+            other = lax.rem(me + d, samp)
+            copy = pltpu.make_async_remote_copy(
+                g.at[pl.ds(pl.multiple_of(p * part_rows + ln * half + other * chunk, 8), chunk)],
+                chunk_in.at[p, d - 1], c_send.at[p, d - 1], c_recv.at[p, d - 1],
+                device_id={"samp": other}, device_id_type=MESH)
+            copy.start()
+            made.append(copy)
+        return made
+
+    def gather(p, scatters):
+        for copy in scatters:
+            copy.wait()
+        own = pl.ds(pl.multiple_of(p * part_rows + ln * half + me * chunk, 8), chunk)
+        value = g[own, :] + corr[own, :]
+        for d in range(1, samp):
+            value = value + chunk_in[p, d - 1]
+        tot[own, :] = value
+        made = []
+        for d in range(1, samp):
+            other = lax.rem(me + d, samp)
+            copy = pltpu.make_async_remote_copy(tot.at[own], tot.at[own], a_send.at[p, d - 1], a_recv.at[p, d - 1],
+                                                device_id={"samp": other}, device_id_type=MESH)
+            copy.start()
+            made.append(copy)
+        return made
+
+    def line_gather(p, gathers):
+        for copy in gathers:
+            copy.wait()
+        mine = pl.ds(pl.multiple_of(p * part_rows + ln * half, 8), half)
+        made = []
+        for d in range(1, line):
+            other = lax.rem(ln + d, line)
+            copy = pltpu.make_async_remote_copy(tot.at[mine], tot.at[mine], b_send.at[p, d - 1], b_recv.at[p, d - 1],
+                                                device_id={"line": other}, device_id_type=MESH)
+            copy.start()
+            made.append(copy)
+        return made
+
+    swaps = []
     for q in range(0, len(rows), 2):
         span = min(2 * LANES, padded - q * LANES)
         both = lax.dot_general(tall[q * LANES:bands], flat_right[q * LANES:q * LANES + span],
                                (((1,), (1,)), ((), ())), preferred_element_type=jnp.float32)
         for b in range(span // LANES):
             g[offsets[q + b]:offsets[q + b] + rows[q + b], :] = both[b * LANES:, b * LANES:(b + 1) * LANES]
-    used = offsets[-1] + rows[-1]
+        if q == 0:
+            swaps.append(line_swap(0))
     if g.shape[0] > used:
         g[used:, :] = jnp.zeros((g.shape[0] - used, LANES), jnp.float32)
-    half = g.shape[0] // line
-    chunk = half // samp
-    copies = []
-    for d in range(1, line):
-        other = lax.rem(ln + d, line)
-        copy = pltpu.make_async_remote_copy(
-            g.at[pl.ds(pl.multiple_of(other * half, 8), half)], half_in.at[d - 1], h_send.at[d - 1],
-            h_recv.at[d - 1], device_id={"line": other}, device_id_type=MESH)
-        copy.start()
-        copies.append(copy)
-    for copy in copies:
-        copy.wait()
-    mine = pl.ds(pl.multiple_of(ln * half, 8), half)
-    value = g[mine, :]
-    for d in range(1, line):
-        value = value + half_in[d - 1]
-    g[mine, :] = value
-    copies = []
-    for d in range(1, samp):
-        other = lax.rem(me + d, samp)
-        copy = pltpu.make_async_remote_copy(
-            g.at[pl.ds(pl.multiple_of(ln * half + other * chunk, 8), chunk)], chunk_in.at[d - 1],
-            c_send.at[d - 1], c_recv.at[d - 1], device_id={"samp": other}, device_id_type=MESH)
-        copy.start()
-        copies.append(copy)
+    swaps.append(line_swap(1))
+    lines1.wait()
+    lift_lines(v1, n1, z1, lines, width, ln, local_mean)
+    rims(z1, lines, width, el1, er1)
+    pair = rim_copies(0, el1, er1, fl1, fr1)
+    scatters = [scatter(p, swaps[p]) for p in range(2)]
     for copy in sum_copies:
         copy.wait()
-    total = sums[...]
-    for d in range(1, devices):
-        total = total + sums_in[d - 1]
-    mean = total / float(pixels * devices)
-    spread = jnp.concatenate([local_mean - mean] + [sums_in[d - 1] / float(pixels) - mean
-                                                    for d in range(1, devices)], axis=0)
+    gathered = jnp.concatenate([sums[...]] + [sums_in[d - 1] for d in range(1, devices)], axis=0)
+    all_lane = lax.broadcasted_iota(jnp.int32, (devices, padded), 1)
+    traces = jnp.sum(gathered[:, padded - 1:padded], axis=0, keepdims=True)
+    means = jnp.where(all_lane < bands, gathered, 0.0) / float(pixels)
+    mean = jnp.sum(means, axis=0, keepdims=True) / float(devices)
+    spread = means - mean
+    trace = traces + float(pixels) * jnp.sum(jnp.sum(spread * spread, axis=0, keepdims=True), axis=1, keepdims=True)
     shift = local_mean - mean
-    for t in range(v1.shape[0]):
-        v1[t] = jnp.transpose(xs[t * LANES:(t + 1) * LANES, :]) + shift[:, t * LANES:(t + 1) * LANES]
-    lines1 = line_copy(0, v1, n1, lines, width)
     for q, (count, offset) in enumerate(zip(rows, offsets)):
         corr[offset:offset + count, :] = float(pixels) * lax.dot_general(
             spread, spread[:, q * LANES:(q + 1) * LANES], (((0,), (0,)), ((), ())), precision=HIGH,
             preferred_element_type=jnp.float32)[q * LANES:q * LANES + count]
     if g.shape[0] > used:
         corr[used:, :] = jnp.zeros((g.shape[0] - used, LANES), jnp.float32)
-    lines1.wait()
-    lift_lines(v1, n1, z1, lines, width, ln)
-    rims(z1, lines, width, el1, er1)
-    for copy in copies:
-        copy.wait()
-    own = pl.ds(pl.multiple_of(ln * half + me * chunk, 8), chunk)
-    value = g[own, :] + corr[own, :]
-    for d in range(1, samp):
-        value = value + chunk_in[d - 1]
-    tot[own, :] = value
-    copies = []
-    for d in range(1, samp):
-        other = lax.rem(me + d, samp)
-        copy = pltpu.make_async_remote_copy(tot.at[own], tot.at[own], a_send.at[d - 1], a_recv.at[d - 1],
-                                            device_id={"samp": other}, device_id_type=MESH)
-        copy.start()
-        copies.append(copy)
-    pair = rim_copies(0, el1, er1, fl1, fr1)
-    for copy in copies:
-        copy.wait()
-    copies = []
-    for d in range(1, line):
-        other = lax.rem(ln + d, line)
-        copy = pltpu.make_async_remote_copy(tot.at[mine], tot.at[mine], b_send.at[d - 1], b_recv.at[d - 1],
-                                            device_id={"line": other}, device_id_type=MESH)
-        copy.start()
-        copies.append(copy)
-    for copy in copies:
+    gathers = [gather(p, scatters[p]) for p in range(2)]
+    h, w = lines // 2, width // 2
+    one = h * w
+    two = one // 4
+    three = two // 4
+    base2, base3 = 3 * one, 3 * one + 3 * two
+    rim_wait(pair)
+    below_shift = sums_in[line - 1] / float(pixels) - local_mean
+    above_shift = sums_in[devices - line - 1] / float(pixels) - local_mean
+    inner = 1.0 + beta_lift * (1.0 + 2.0 * alpha_lift)
+    for t in range(v1.shape[0]):
+        part = slice(t * LANES, (t + 1) * LANES)
+        low_half = slice(0, lines // 2)
+        next_half = slice(lines, lines + lines // 2)
+        fl1[t, low_half] = fl1[t, low_half] + below_shift[:, part] * (1.0 + alpha_lift)
+        fl1[t, next_half] = fl1[t, next_half] + below_shift[:, part] * inner
+        fr1[t, low_half] = fr1[t, low_half] + above_shift[:, part]
+        fr1[t, next_half] = fr1[t, next_half] + above_shift[:, part] * inner
+    lift_samples(z1, fl1, fr1, lines, width, first, last, ((v2, 0), (t_ref, 0), (t_ref, one), (t_ref, 2 * one)))
+    for t in range(v1.shape[0]):
+        v2[t] = v2[t] + shift[:, t * LANES:(t + 1) * LANES]
+    lines2 = line_copy(1, v2, n2, h, w)
+    closing = line_gather(0, gathers[0])
+    lines2.wait()
+    lift_lines(v2, n2, z2, h, w, ln)
+    rims(z2, h, w, el2, er2)
+    pair2 = rim_copies(1, el2, er2, fl2, fr2)
+    for copy in closing:
         copy.wait()
     wide = m.shape[1]
-    rows, offsets = blocks_of(bands)
     diag = lax.broadcasted_iota(jnp.int32, (LANES, LANES), 0) == lax.broadcasted_iota(
         jnp.int32, (LANES, LANES), 1)
     scale = 1.0 / float(pixels * devices)
-    trace = jnp.zeros((1, 1), jnp.float32)
-    for q, offset in enumerate(offsets):
-        size = min(LANES, rows[q])
-        block = tot[offset:offset + size, :]
-        kept = jnp.where(diag[:size], block, 0.0)
-        trace = trace + jnp.sum(jnp.sum(kept, axis=0, keepdims=True), axis=1, keepdims=True)
     ridge = trace * scale * (0.01 / bands)
-    for q, offset in enumerate(offsets):
+
+    def place(q, fresh):
+        offset = offsets[q]
         for b in range(q, len(rows)):
             size = min(LANES, rows[b])
             start = offset + (b - q) * LANES
             block = tot[start:start + size, :] * scale
+            row_part, col_part = slice(q * LANES, q * LANES + size), slice(q * LANES, (q + 1) * LANES)
             if b == q:
                 low = jnp.where(diag[:size], block + ridge, block)
-                m[q * LANES:q * LANES + size, q * LANES:(q + 1) * LANES] = low
+                m[row_part, col_part] = low if fresh else m[row_part, col_part] + low
             else:
                 if size < LANES:
                     block = jnp.concatenate([block, jnp.zeros((LANES - size, LANES), jnp.float32)], axis=0)
-                m[q * LANES:(q + 1) * LANES, b * LANES:(b + 1) * LANES] = jnp.transpose(block)
-                m[b * LANES:b * LANES + size, q * LANES:(q + 1) * LANES] = block[:size]
+                upper_rows, upper_cols = slice(q * LANES, (q + 1) * LANES), slice(b * LANES, (b + 1) * LANES)
+                lower_rows = slice(b * LANES, b * LANES + size)
+                flipped = jnp.transpose(block)
+                if fresh:
+                    m[upper_rows, upper_cols] = flipped
+                    m[lower_rows, col_part] = block[:size]
+                else:
+                    m[upper_rows, upper_cols] = m[upper_rows, upper_cols] + flipped
+                    m[lower_rows, col_part] = m[lower_rows, col_part] + block[:size]
+
+    place(0, True)
+    m[LANES:, LANES:] = jnp.zeros((bands - LANES, wide - LANES), jnp.float32)
     sub = lax.broadcasted_iota(jnp.int32, (8, LANES), 0)
     lane = lax.broadcasted_iota(jnp.int32, (8, LANES), 1)
     tiles = wide // LANES
@@ -380,37 +444,26 @@
                         old = jnp.where((lanes >= start % LANES) & (lanes < start % LANES + size), 0.0, old)
                     m[low_row:high_row, u * LANES:(u + 1) * LANES] = old - update[:, u * LANES:(u + 1) * LANES]
 
-    h, w = lines // 2, width // 2
-    one = h * w
-    two = one // 4
-    three = two // 4
-    base2, base3 = 3 * one, 3 * one + 3 * two
     state = {}
 
-    def stage0():
-        rim_wait(pair)
-        lift_samples(z1, fl1, fr1, lines, width, first, last, ((v2, 0), (t_ref, 0), (t_ref, one), (t_ref, 2 * one)))
-        state["lines"] = line_copy(1, v2, n2, h, w)
-
-    def stage1():
-        state["lines"].wait()
-        lift_lines(v2, n2, z2, h, w, ln)
-        rims(z2, h, w, el2, er2)
-        state["pair"] = rim_copies(1, el2, er2, fl2, fr2)
-
-    def stage2():
-        rim_wait(state["pair"])
+    def stage_rest():
+        closing = line_gather(1, gathers[1])
+        rim_wait(pair2)
         lift_samples(z2, fl2, fr2, h, w, first, last,
                      ((v3, 0), (t_ref, base2), (t_ref, base2 + two), (t_ref, base2 + 2 * two)))
         state["lines"] = line_copy(2, v3, n3, h // 2, w // 2)
-
-    def stage3():
+        for copy in closing:
+            copy.wait()
+        for q in range(1, len(rows)):
+            place(q, False)
+
+    def stage0():
         state["lines"].wait()
         lift_lines(v3, n3, z3, h // 2, w // 2, ln)
         rims(z3, h // 2, w // 2, el3, er3)
         state["pair"] = rim_copies(2, el3, er3, fl3, fr3)
 
-    def stage4():
+    def stage1():
         rim_wait(state["pair"])
         lift_samples(z3, fl3, fr3, h // 2, w // 2, first, last,
                      ((t_ref, base3 + 3 * three), (t_ref, base3), (t_ref, base3 + three), (t_ref, base3 + 2 * three)))
@@ -454,12 +507,12 @@
             pack(o3_ref, i * (o3_ref.shape[0] // 3), 3 * two + i * three, three, low_row, count)
         pack(o4_ref, 0, 3 * two + 3 * three, three, low_row, count)
 
-    stages = [stage0, stage1, stage2, stage3, stage4]
+    stages = {LANES // SUPER - 1: stage_rest, LANES // SUPER: stage0, LANES // SUPER + 2: stage1}
     ready = 0
     for start in range(0, bands, SUPER):
         superblock(start)
-        if stages:
-            stages.pop(0)()
+        if start // SUPER in stages:
+            stages.pop(start // SUPER)()
         if not stages:
             while ready * LANES < bands and min(bands, (ready + 1) * LANES) <= start + SUPER:
                 final(ready)
@@ -492,7 +545,7 @@
     devices = samp * line
     rows, offsets = blocks_of(bands)
     used = offsets[-1] + rows[-1]
-    unit = 8 * devices
+    unit = 16 * devices
     total = -(-used // unit) * unit
     padded = -(-bands // LANES) * LANES
     f32 = jnp.float32
@@ -518,11 +571,11 @@
             sem((3,)), sem((3,)), sem((3, 2)), sem((3, 2)),
             pltpu.VMEM((padded, pixels), f32), pltpu.VMEM((1, padded), f32),
             pltpu.VMEM((devices - 1, 1, padded), f32), pltpu.VMEM((total, LANES), f32),
-            pltpu.VMEM((line - 1, total // line, LANES), f32),
-            pltpu.VMEM((samp - 1, total // devices, LANES), f32), pltpu.VMEM((total, LANES), f32),
-            sem((devices - 1,)), sem((devices - 1,)), sem((line - 1,)), sem((line - 1,)),
-            sem((samp - 1,)), sem((samp - 1,)), sem((samp - 1,)), sem((samp - 1,)),
-            sem((line - 1,)), sem((line - 1,)),
+            pltpu.VMEM((2, line - 1, total // 2 // line, LANES), f32),
+            pltpu.VMEM((2, samp - 1, total // 2 // devices, LANES), f32), pltpu.VMEM((total, LANES), f32),
+            sem((devices - 1,)), sem((devices - 1,)), sem((2, line - 1)), sem((2, line - 1)),
+            sem((2, samp - 1)), sem((2, samp - 1)), sem((2, samp - 1)), sem((2, samp - 1)),
+            sem((2, line - 1)), sem((2, line - 1)),
         ],
         compiler_params=pltpu.CompilerParams(collective_id=0, has_side_effects=True,
                                              vmem_limit_bytes=32 * 1024 * 1024),

time: 44.2 us -> 41.1 us (0.930)
  Pallas kernels: 42.2 us -> 39.1 us
    pallas_call x1, Pallas kernels: 41.3 us -> 38.2 us  [gram_call(): pl.pallas_call(functools.partial(gram_kernel, samp, line, bands, lines, w...]
where the time goes in v3:
time: 41.1 us; the launch traced here: 40.9 us
  Pallas kernels  39.1 us (95%)
  local copies, waits for them, and re-layouts  1.16 us (3%)
  between operations  0.65 us (2%)
    pallas_call x1, Pallas kernels, gram_call(): pl.pallas_call(functools.partial(gram_kernel, samp, line, bands, lines, w...  38.2 us
    unnamed x2, local copies, waits for them, and re-layouts  1.16 us
    pallas_call x1, Pallas kernels, store_call(): pl.pallas_call(store_kernel, out_shape=tuple((jax.ShapeDtypeStruct(a.shap...  0.93 us

profile of v3, /device:TPU:0, one launch (start us, length us, event | category | flops | bytes accessed | tf_op | source)
XLA Modules:
  0.0 40.9 jit_solution(14033688621274721593)
XLA Ops:
  0.6 0.0 copy-start
  0.6 1.2 %copy-done = f32[221184]{0:T(1024)S(1)} copy-done((f32[221184]{0:T(1024)S(1)}, f32[221184]{0:T(1024)}, u32[]{:S(2)}) %copy-start) | copy-done | bytes 884760
  1.8 38.2 %shard_map.46 = (f32[3,432,128]{2,1,0:T(8,128)S(1)}, f32[324,128]{1,0:T(8,128)S(1)}, f32[81,128]{1,0:T(8,128)S(1)}, f32[27,128]{1,0:T(8,128)S(1)}) custom-call(f32[1728,128]{1,0:T(8,128)S(1)} %bitcast.5), custom_call_target="tpu_custom_call" | custom-call | tf_op jit(solution)/shard_map/pallas_call | solution.py:553
  40.0 0.9 %shard_map.47 = (f32[3,432,128]{2,1,0:T(8,128)}, f32[324,128]{1,0:T(8,128)}, f32[81,128]{1,0:T(8,128)}, f32[27,128]{1,0:T(8,128)}) custom-call(f32[3,432,128]{2,1,0:T(8,128)S(1)} %get-tuple-element.12.refs_0_, f32[324,128]{1,0:T(8,128)S(1)} %get-tuple-element.13.refs_1_, f32[81,128]{1,0:T(8,128)S(1)} %get-tuple-element.14.refs_2_, ...), custom_call_target="tpu_custom_call" | custom-call | tf_op jit(solution)/shard_map/pallas_call | solution.py:532
Async XLA Ops:
  0.6 1.2 %copy-start = (f32[221184]{0:T(1024)S(1)}, f32[221184]{0:T(1024)}, u32[]{:S(2)}) copy-start(f32[221184]{0:T(1024)} %param.1) | copy-start | bytes 2654212

commit v4 on v3

--- a/solution.py
+++ b/solution.py
@@ -14,6 +14,7 @@
 HIGH = lax.Precision.HIGHEST
 LANES = 128
 SUPER = 64
+CSTAGE = 3
 
 
 def blocks_of(bands):
@@ -175,15 +176,6 @@
     energy = jnp.sum(jnp.sum(energy, axis=0, keepdims=True), axis=1, keepdims=True)
     sum_lane = lax.broadcasted_iota(jnp.int32, (1, padded), 1)
     sums[...] = jnp.where(sum_lane < bands, row_sums, energy)
-    pl.semaphore_wait(barrier, devices - 1)
-    lines1 = line_copy(0, v1, n1, lines, width)
-    copies = []
-    for d in range(1, devices):
-        copy = pltpu.make_async_remote_copy(sums, sums_in.at[d - 1], s_send.at[d - 1], s_recv.at[d - 1],
-                                            device_id=peer(d), device_id_type=MESH)
-        copy.start()
-        copies.append(copy)
-    sum_copies = copies
     local_mean = row_sums / float(pixels)
     coarse = [part.astype(jnp.bfloat16) for part in parts]
     fine = [(part - top_part.astype(jnp.float32)).astype(jnp.bfloat16) for part, top_part in zip(parts, coarse)]
@@ -253,23 +245,29 @@
             made.append(copy)
         return made
 
-    swaps = []
     for q in range(0, len(rows), 2):
         span = min(2 * LANES, padded - q * LANES)
         both = lax.dot_general(tall[q * LANES:bands], flat_right[q * LANES:q * LANES + span],
                                (((1,), (1,)), ((), ())), preferred_element_type=jnp.float32)
         for b in range(span // LANES):
             g[offsets[q + b]:offsets[q + b] + rows[q + b], :] = both[b * LANES:, b * LANES:(b + 1) * LANES]
-        if q == 0:
-            swaps.append(line_swap(0))
     if g.shape[0] > used:
         g[used:, :] = jnp.zeros((g.shape[0] - used, LANES), jnp.float32)
+    pl.semaphore_wait(barrier, devices - 1)
+    copies = []
+    for d in range(1, devices):
+        copy = pltpu.make_async_remote_copy(sums, sums_in.at[d - 1], s_send.at[d - 1], s_recv.at[d - 1],
+                                            device_id=peer(d), device_id_type=MESH)
+        copy.start()
+        copies.append(copy)
+    sum_copies = copies
+    swaps = [line_swap(0)]
+    lines1 = line_copy(0, v1, n1, lines, width)
     swaps.append(line_swap(1))
+    scatters = [scatter(p, swaps[p]) for p in range(2)]
     lines1.wait()
     lift_lines(v1, n1, z1, lines, width, ln, local_mean)
     rims(z1, lines, width, el1, er1)
-    pair = rim_copies(0, el1, er1, fl1, fr1)
-    scatters = [scatter(p, swaps[p]) for p in range(2)]
     for copy in sum_copies:
         copy.wait()
     gathered = jnp.concatenate([sums[...]] + [sums_in[d - 1] for d in range(1, devices)], axis=0)
@@ -286,33 +284,15 @@
             preferred_element_type=jnp.float32)[q * LANES:q * LANES + count]
     if g.shape[0] > used:
         corr[used:, :] = jnp.zeros((g.shape[0] - used, LANES), jnp.float32)
-    gathers = [gather(p, scatters[p]) for p in range(2)]
+    gathers = [gather(0, scatters[0])]
+    pair = rim_copies(0, el1, er1, fl1, fr1)
+    gathers.append(gather(1, scatters[1]))
     h, w = lines // 2, width // 2
     one = h * w
     two = one // 4
     three = two // 4
     base2, base3 = 3 * one, 3 * one + 3 * two
-    rim_wait(pair)
-    below_shift = sums_in[line - 1] / float(pixels) - local_mean
-    above_shift = sums_in[devices - line - 1] / float(pixels) - local_mean
-    inner = 1.0 + beta_lift * (1.0 + 2.0 * alpha_lift)
-    for t in range(v1.shape[0]):
-        part = slice(t * LANES, (t + 1) * LANES)
-        low_half = slice(0, lines // 2)
-        next_half = slice(lines, lines + lines // 2)
-        fl1[t, low_half] = fl1[t, low_half] + below_shift[:, part] * (1.0 + alpha_lift)
-        fl1[t, next_half] = fl1[t, next_half] + below_shift[:, part] * inner
-        fr1[t, low_half] = fr1[t, low_half] + above_shift[:, part]
-        fr1[t, next_half] = fr1[t, next_half] + above_shift[:, part] * inner
-    lift_samples(z1, fl1, fr1, lines, width, first, last, ((v2, 0), (t_ref, 0), (t_ref, one), (t_ref, 2 * one)))
-    for t in range(v1.shape[0]):
-        v2[t] = v2[t] + shift[:, t * LANES:(t + 1) * LANES]
-    lines2 = line_copy(1, v2, n2, h, w)
     closing = line_gather(0, gathers[0])
-    lines2.wait()
-    lift_lines(v2, n2, z2, h, w, ln)
-    rims(z2, h, w, el2, er2)
-    pair2 = rim_copies(1, el2, er2, fl2, fr2)
     for copy in closing:
         copy.wait()
     wide = m.shape[1]
@@ -446,18 +426,52 @@
 
     state = {}
 
+    def convert(low_pix, high_pix):
+        for t in range(tiles):
+            top_part = t_ref[t, low_pix:high_pix].astype(jnp.bfloat16)
+            th[t, low_pix:high_pix] = top_part
+            tl[t, low_pix:high_pix] = (t_ref[t, low_pix:high_pix] - top_part.astype(jnp.float32)).astype(jnp.bfloat16)
+
+    def stage_a():
+        rim_wait(pair)
+        below_shift = sums_in[line - 1] / float(pixels) - local_mean
+        above_shift = sums_in[devices - line - 1] / float(pixels) - local_mean
+        inner = 1.0 + beta_lift * (1.0 + 2.0 * alpha_lift)
+        for t in range(v1.shape[0]):
+            part = slice(t * LANES, (t + 1) * LANES)
+            low_half = slice(0, lines // 2)
+            next_half = slice(lines, lines + lines // 2)
+            fl1[t, low_half] = fl1[t, low_half] + below_shift[:, part] * (1.0 + alpha_lift)
+            fl1[t, next_half] = fl1[t, next_half] + below_shift[:, part] * inner
+            fr1[t, low_half] = fr1[t, low_half] + above_shift[:, part]
+            fr1[t, next_half] = fr1[t, next_half] + above_shift[:, part] * inner
+        lift_samples(z1, fl1, fr1, lines, width, first, last, ((v2, 0), (t_ref, 0), (t_ref, one), (t_ref, 2 * one)))
+        for t in range(v1.shape[0]):
+            v2[t] = v2[t] + shift[:, t * LANES:(t + 1) * LANES]
+        state["lines"] = line_copy(1, v2, n2, h, w)
+        convert(0, 256)
+
     def stage_rest():
         closing = line_gather(1, gathers[1])
-        rim_wait(pair2)
-        lift_samples(z2, fl2, fr2, h, w, first, last,
-                     ((v3, 0), (t_ref, base2), (t_ref, base2 + two), (t_ref, base2 + 2 * two)))
-        state["lines"] = line_copy(2, v3, n3, h // 2, w // 2)
+        stage_b()
         for copy in closing:
             copy.wait()
         for q in range(1, len(rows)):
             place(q, False)
 
-    def stage0():
+    def stage_b():
+        state["lines"].wait()
+        lift_lines(v2, n2, z2, h, w, ln)
+        rims(z2, h, w, el2, er2)
+        state["pair"] = rim_copies(1, el2, er2, fl2, fr2)
+
+    def stage_c():
+        rim_wait(state["pair"])
+        lift_samples(z2, fl2, fr2, h, w, first, last,
+                     ((v3, 0), (t_ref, base2), (t_ref, base2 + two), (t_ref, base2 + 2 * two)))
+        state["lines"] = line_copy(2, v3, n3, h // 2, w // 2)
+
+    def stage_d():
         state["lines"].wait()
         lift_lines(v3, n3, z3, h // 2, w // 2, ln)
         rims(z3, h // 2, w // 2, el3, er3)
@@ -467,10 +481,7 @@
         rim_wait(state["pair"])
         lift_samples(z3, fl3, fr3, h // 2, w // 2, first, last,
                      ((t_ref, base3 + 3 * three), (t_ref, base3), (t_ref, base3 + three), (t_ref, base3 + 2 * three)))
-        for t in range(tiles):
-            top_part = t_ref[t].astype(jnp.bfloat16)
-            th[t] = top_part
-            tl[t] = (t_ref[t] - top_part.astype(jnp.float32)).astype(jnp.bfloat16)
+        convert(256 if t_ref.shape[1] > 256 else 0, t_ref.shape[1])
 
     def pack(dest, at, lane0, wide_out, low_row, count):
         group = LANES // wide_out
@@ -479,7 +490,7 @@
         at = at + low_row // group
         dest[at:at + count // group, :] = jnp.concatenate(pieces, axis=1)
 
-    def final(r):
+    def final(r, first_part, last_part):
         low_row = r * LANES
         count = min(LANES, bands - low_row)
         keep = lax.broadcasted_iota(jnp.int32, (count, LANES), 1) <= lax.broadcasted_iota(jnp.int32, (count, LANES), 0)
@@ -490,7 +501,7 @@
         lower = (whole - upper.astype(jnp.float32)).astype(jnp.bfloat16)
         left = jnp.concatenate([upper, lower, upper], axis=1)
         chunks = t_ref.shape[1] // LANES
-        for q in range(0, chunks, 2):
+        for q in range(0 if first_part else 2, chunks if last_part else 2, 2):
             pix = slice(q * LANES, min(q + 2, chunks) * LANES)
             big = [th[t, pix, :] for t in range(r + 1)]
             small = [tl[t, pix, :] for t in range(r + 1)]
@@ -502,21 +513,25 @@
                     o1_ref[q + b, low_row:low_row + count, :] = part
                 else:
                     rest[low_row:low_row + count, :] = part
+        if not last_part:
+            return
         for i in range(3):
             pack(o2_ref, i * (o2_ref.shape[0] // 3), i * two, two, low_row, count)
             pack(o3_ref, i * (o3_ref.shape[0] // 3), 3 * two + i * three, three, low_row, count)
         pack(o4_ref, 0, 3 * two + 3 * three, three, low_row, count)
 
-    stages = {LANES // SUPER - 1: stage_rest, LANES // SUPER: stage0, LANES // SUPER + 2: stage1}
-    ready = 0
+    stages = {0: stage_a, 1: stage_rest, CSTAGE: stage_c, CSTAGE + 1: stage_d}
     for start in range(0, bands, SUPER):
         superblock(start)
         if start // SUPER in stages:
             stages.pop(start // SUPER)()
-        if not stages:
-            while ready * LANES < bands and min(bands, (ready + 1) * LANES) <= start + SUPER:
-                final(ready)
-                ready += 1
+    for key in sorted(stages):
+        stages[key]()
+    for r in range(len(rows)):
+        final(r, True, False)
+    stage1()
+    for r in range(len(rows)):
+        final(r, False, True)
 
 
 def store_kernel(*refs):

time: 41.1 us -> 39 us (0.949)
  Pallas kernels: 39.1 us -> 36.8 us
    pallas_call x1, Pallas kernels: 38.2 us -> 35.9 us  [gram_call(): pl.pallas_call(functools.partial(gram_kernel, samp, line, bands, lines, w...]
where the time goes in v4:
time: 39 us; the launch traced here: 38.8 us
  Pallas kernels  36.8 us (94%)
  local copies, waits for them, and re-layouts  1.16 us (3%)
  between operations  0.81 us (2%)
    pallas_call x1, Pallas kernels, gram_call(): pl.pallas_call(functools.partial(gram_kernel, samp, line, bands, lines, w...  35.9 us
    unnamed x2, local copies, waits for them, and re-layouts  1.16 us
    pallas_call x1, Pallas kernels, store_call(): pl.pallas_call(store_kernel, out_shape=tuple((jax.ShapeDtypeStruct(a.shap...  0.93 us

profile of v4, /device:TPU:0, one launch (start us, length us, event | category | flops | bytes accessed | tf_op | source)
XLA Modules:
  0.0 38.8 jit_solution(13595436757384330245)
XLA Ops:
  0.6 0.0 copy-start
  0.6 1.2 %copy-done = f32[221184]{0:T(1024)S(1)} copy-done((f32[221184]{0:T(1024)S(1)}, f32[221184]{0:T(1024)}, u32[]{:S(2)}) %copy-start) | copy-done | bytes 884760
  1.8 35.9 %shard_map.46 = (f32[3,432,128]{2,1,0:T(8,128)S(1)}, f32[324,128]{1,0:T(8,128)S(1)}, f32[81,128]{1,0:T(8,128)S(1)}, f32[27,128]{1,0:T(8,128)S(1)}) custom-call(f32[1728,128]{1,0:T(8,128)S(1)} %bitcast.5), custom_call_target="tpu_custom_call" | custom-call | tf_op jit(solution)/shard_map/pallas_call | solution.py:568
  37.7 0.9 %shard_map.47 = (f32[3,432,128]{2,1,0:T(8,128)}, f32[324,128]{1,0:T(8,128)}, f32[81,128]{1,0:T(8,128)}, f32[27,128]{1,0:T(8,128)}) custom-call(f32[3,432,128]{2,1,0:T(8,128)S(1)} %get-tuple-element.12.refs_0_, f32[324,128]{1,0:T(8,128)S(1)} %get-tuple-element.13.refs_1_, f32[81,128]{1,0:T(8,128)S(1)} %get-tuple-element.14.refs_2_, ...), custom_call_target="tpu_custom_call" | custom-call | tf_op jit(solution)/shard_map/pallas_call | solution.py:547
Async XLA Ops:
  0.6 1.2 %copy-start = (f32[221184]{0:T(1024)S(1)}, f32[221184]{0:T(1024)}, u32[]{:S(2)}) copy-start(f32[221184]{0:T(1024)} %param.1) | copy-start | bytes 2654212

commit v5 on v4

--- a/solution.py
+++ b/solution.py
@@ -280,8 +280,8 @@
     shift = local_mean - mean
     for q, (count, offset) in enumerate(zip(rows, offsets)):
         corr[offset:offset + count, :] = float(pixels) * lax.dot_general(
-            spread, spread[:, q * LANES:(q + 1) * LANES], (((0,), (0,)), ((), ())), precision=HIGH,
-            preferred_element_type=jnp.float32)[q * LANES:q * LANES + count]
+            spread[:, q * LANES:], spread[:, q * LANES:(q + 1) * LANES], (((0,), (0,)), ((), ())), precision=HIGH,
+            preferred_element_type=jnp.float32)[0:count]
     if g.shape[0] > used:
         corr[used:, :] = jnp.zeros((g.shape[0] - used, LANES), jnp.float32)
     gathers = [gather(0, scatters[0])]

time: 39 us -> 39.1 us (level)
  no operation moved by 1% of the time
where the time goes in v5:
time: 39.1 us; the launch traced here: 38.9 us
  Pallas kernels  36.9 us (94%)
  local copies, waits for them, and re-layouts  1.16 us (3%)
  between operations  0.81 us (2%)
    pallas_call x1, Pallas kernels, gram_call(): pl.pallas_call(functools.partial(gram_kernel, samp, line, bands, lines, w...  36 us
    unnamed x2, local copies, waits for them, and re-layouts  1.16 us
    pallas_call x1, Pallas kernels, store_call(): pl.pallas_call(store_kernel, out_shape=tuple((jax.ShapeDtypeStruct(a.shap...  0.93 us

profile of v5, /device:TPU:0, one launch (start us, length us, event | category | flops | bytes accessed | tf_op | source)
XLA Modules:
  0.0 38.9 jit_solution(1462566202396983645)
XLA Ops:
  0.6 0.0 copy-start
  0.6 1.2 %copy-done = f32[221184]{0:T(1024)S(1)} copy-done((f32[221184]{0:T(1024)S(1)}, f32[221184]{0:T(1024)}, u32[]{:S(2)}) %copy-start) | copy-done | bytes 884760
  1.8 36.0 %shard_map.46 = (f32[3,432,128]{2,1,0:T(8,128)S(1)}, f32[324,128]{1,0:T(8,128)S(1)}, f32[81,128]{1,0:T(8,128)S(1)}, f32[27,128]{1,0:T(8,128)S(1)}) custom-call(f32[1728,128]{1,0:T(8,128)S(1)} %bitcast.5), custom_call_target="tpu_custom_call" | custom-call | tf_op jit(solution)/shard_map/pallas_call | solution.py:568
  37.8 0.9 %shard_map.47 = (f32[3,432,128]{2,1,0:T(8,128)}, f32[324,128]{1,0:T(8,128)}, f32[81,128]{1,0:T(8,128)}, f32[27,128]{1,0:T(8,128)}) custom-call(f32[3,432,128]{2,1,0:T(8,128)S(1)} %get-tuple-element.12.refs_0_, f32[324,128]{1,0:T(8,128)S(1)} %get-tuple-element.13.refs_1_, f32[81,128]{1,0:T(8,128)S(1)} %get-tuple-element.14.refs_2_, ...), custom_call_target="tpu_custom_call" | custom-call | tf_op jit(solution)/shard_map/pallas_call | solution.py:547
Async XLA Ops:
  0.6 1.2 %copy-start = (f32[221184]{0:T(1024)S(1)}, f32[221184]{0:T(1024)}, u32[]{:S(2)}) copy-start(f32[221184]{0:T(1024)} %param.1) | copy-start | bytes 2654212
